TPU v7x, 256 devices: a whole 4x4x8 slice. The times are simulated.
256 devices in a mesh: tm: 128 (over y, x, z), det: 2 (over core).
Axes of the slice: x: 4, y: 4, z: 8, core: 2. Of those that a mesh axis runs over, the one named last changes fastest.
Arguments:
- offset_coeffs: float32 [16, 256], P('det', 'tm'), may hold values from -6 to 6
- leftover_error: float32 [16, 256], P('det', 'tm'), may hold values from -22 to 22
- search_vector: float32 [16, 256], P('det', 'tm'), may hold values from -22 to 22
- node_lattice_offset: int32 [16], P('det'), may hold values from 0 to 1023
- sky_cell_in_patch: int32 [16, 262144], P('det', 'tm'), may hold values from 0 to 127
- analyser_reading_phase: float32 [16, 262144], P('det', 'tm'), may hold values from -3.140625 to 3.140625
- segment_sky_patch: int32 [16, 2048], P('det', 'tm'), may hold values from 0 to 131071, as said below
Outputs:
- fresh_offset_coeffs: float32 [16, 256], P('det', 'tm')
- fresh_leftover_error: float32 [16, 256], P('det', 'tm')
- fresh_search_vector: float32 [16, 256], P('det', 'tm')
Inputs may be any that keep to these rules, and one draw needn't show every extreme that they name: `segment_sky_patch`: tile t belongs to owner t // 1024. Among the blocks of one device (8 detectors, one time span), at most 2 lie in tiles of one owner, and on every device some owner holds exactly 2 of them.
All inputs are finite; a program needn't handle non-finite values.
Results may differ from a plain program's by a relative error of at most 0.0001.
Values sent between devices are 32-bit elements; how exact they have to be, the bound alone decides.
A program may use at most 64 MiB of HBM per device.

v0:
```python
import math

import jax
import jax.numpy as jnp
from jax import lax
from jax.sharding import PartitionSpec as P

PIX_OWN = 131072


MAP_PRIOR = 1.0
BASE_PRIOR = 0.1
LANES = 128


def padded_2(cells, sides, width):
    for axis, dim in sides:
        count = lax.axis_size(axis)
        head = lax.slice_in_dim(cells, 0, width, axis=dim)
        tail = lax.slice_in_dim(cells, cells.shape[dim] - width, cells.shape[dim], axis=dim)
        cells = jnp.concatenate(
            [
                lax.ppermute(tail, axis, [(i, (i + 1) % count) for i in range(count)]),
                cells,
                lax.ppermute(head, axis, [((i + 1) % count, i) for i in range(count)]),
            ],
            axis=dim,
        )
    return cells


def spline_weights(fraction):
    square = fraction * fraction
    cube = square * fraction
    first = (1.0 - fraction) * (1.0 - fraction) * (1.0 - fraction) / 6.0
    second = (3.0 * cube - 6.0 * square + 4.0) / 6.0
    third = (-3.0 * cube + 3.0 * square + 3.0 * fraction + 1.0) / 6.0
    fourth = cube / 6.0
    return (first, second, third, fourth)


def solve_pixels(sums):
    total_signal, signal_cos, signal_sin, hit_count, cos_sum, sin_sum, cos_cos, cos_sin, sin_sin = (
        sums
    )
    stokes_i = hit_count + MAP_PRIOR
    stokes_q = cos_cos + MAP_PRIOR
    stokes_u = sin_sin + MAP_PRIOR
    minor_one = stokes_q * stokes_u - cos_sin * cos_sin
    minor_two = sin_sum * cos_sin - cos_sum * stokes_u
    minor_three = cos_sum * cos_sin - sin_sum * stokes_q
    minor_four = stokes_i * stokes_u - sin_sum * sin_sum
    minor_five = cos_sum * sin_sum - stokes_i * cos_sin
    minor_six = stokes_i * stokes_q - cos_sum * cos_sum
    determinant = stokes_i * minor_one + cos_sum * minor_two + sin_sum * minor_three
    intensity = (
        minor_one * total_signal + minor_two * signal_cos + minor_three * signal_sin
    ) / determinant
    polar_q = (
        minor_two * total_signal + minor_four * signal_cos + minor_five * signal_sin
    ) / determinant
    polar_u = (
        minor_three * total_signal + minor_five * signal_cos + minor_six * signal_sin
    ) / determinant
    return (intensity, polar_q, polar_u)


def solve_tiles(sums):
    parts = tuple((sums[:, column] for column in range(9)))
    return jnp.stack(solve_pixels(parts), axis=1)


def place_rows(rows, labels, owner_tiles):
    targets = labels.astype(jnp.int32)
    targets = jnp.where(targets < 0, owner_tiles, targets)
    return jnp.zeros((owner_tiles + 1, 9, LANES), jnp.float32).at[targets].add(rows)[:owner_tiles]


def combine_maps(rows, labels, owner_tiles):
    partial_value = place_rows(rows, labels, owner_tiles)
    totals = lax.psum(partial_value, "det")
    return solve_tiles(totals)


def block_groups(block_count):
    return math.gcd(block_count, 64)


def bin_blocks(entries, offsets):
    block_count, channels = (entries.shape[0], entries.shape[1])
    group_width = block_groups(block_count)
    lane_ids = jnp.arange(LANES, dtype=jnp.int32)

    def bin_one_group(input_arrays):
        indicator_matrix = (input_arrays[1][:, :, None] == lane_ids[None, None, :]).astype(
            jnp.float32
        )
        return jnp.einsum(
            "zte,zeh->zth", input_arrays[0], indicator_matrix, precision=lax.Precision.HIGHEST
        )

    binned = lax.map(
        bin_one_group,
        (
            entries.reshape(block_count // group_width, group_width, channels, LANES),
            offsets.reshape(block_count // group_width, group_width, LANES),
        ),
    )
    return binned.reshape(block_count, channels, LANES)


def read_blocks(tile_maps, offsets):
    block_count, channels = (tile_maps.shape[0], tile_maps.shape[1])
    group_width = block_groups(block_count)
    lane_ids = jnp.arange(LANES, dtype=jnp.int32)

    def read_one_group(input_arrays):
        indicator_matrix = (input_arrays[1][:, :, None] == lane_ids[None, None, :]).astype(
            jnp.float32
        )
        return jnp.einsum(
            "rhe,roe->rho", input_arrays[0], indicator_matrix, precision=lax.Precision.HIGHEST
        )

    values_read = lax.map(
        read_one_group,
        (
            tile_maps.reshape(block_count // group_width, group_width, channels, LANES),
            offsets.reshape(block_count // group_width, group_width, LANES),
        ),
    )
    return values_read.reshape(block_count, channels, LANES)


def pixel_sums(stream_blocks, cos_blocks, sin_blocks):
    ones = jnp.ones_like(cos_blocks)
    return jnp.stack(
        [
            stream_blocks,
            stream_blocks * cos_blocks,
            stream_blocks * sin_blocks,
            ones,
            cos_blocks,
            sin_blocks,
            cos_blocks * cos_blocks,
            cos_blocks * sin_blocks,
            sin_blocks * sin_blocks,
        ],
        axis=1,
    )


def body(
    offset_coeffs,
    leftover_error,
    search_vector,
    node_lattice_offset,
    sky_cell_in_patch,
    analyser_reading_phase,
    segment_sky_patch,
):
    ranks = lax.axis_size("tm")
    tm_index = lax.axis_index("tm")
    det_count, samples = analyser_reading_phase.shape
    node_portion = offset_coeffs.shape[1]
    spacing = samples // node_portion
    width_ext = node_portion + 4
    times = tm_index * samples + jnp.arange(samples, dtype=jnp.int32)
    shifted = times[None, :] - node_lattice_offset[:, None]
    interval = jnp.floor_divide(shifted, spacing)
    fraction = (shifted - interval * spacing).astype(jnp.float32) / spacing
    weights = spline_weights(fraction)
    local_knot = interval - tm_index * node_portion
    columns = []
    for column in range(width_ext):
        weight_col = jnp.zeros_like(fraction)
        for term in range(4):
            weight_col = weight_col + jnp.where(local_knot + term + 1 == column, weights[term], 0.0)
        columns.append(weight_col)
    extended = padded_2(search_vector, (("tm", 1),), 2)
    stream = jnp.zeros_like(fraction)
    for column in range(width_ext):
        stream = stream + columns[column] * extended[:, column : column + 1]
    cosine = jnp.cos(2.0 * analyser_reading_phase)
    sine = jnp.sin(2.0 * analyser_reading_phase)
    block_count = segment_sky_patch.size
    offsets = sky_cell_in_patch.reshape(block_count, LANES)
    stream_blocks = stream.reshape(block_count, LANES)
    cos_blocks = cosine.reshape(block_count, LANES)
    sin_blocks = sine.reshape(block_count, LANES)
    tiles = segment_sky_patch.reshape(block_count)
    owner_tiles = PIX_OWN // LANES
    owners = tiles // owner_tiles
    local_tiles = tiles - owners * owner_tiles
    capacity = max(2, 2 * block_count // ranks)
    slot_total = ranks * capacity
    member = (owners[:, None] == jnp.arange(ranks, dtype=jnp.int32)[None, :]).astype(jnp.int32)
    earlier = jnp.cumsum(member, axis=0) - member
    slots = owners * capacity + jnp.sum(earlier * member, axis=1)
    labels = (
        jnp.full((slot_total,), -1.0, jnp.float32).at[slots].set(local_tiles.astype(jnp.float32))
    )
    labels = labels.reshape(ranks, capacity)
    binned = bin_blocks(pixel_sums(stream_blocks, cos_blocks, sin_blocks), offsets)
    outgoing = jnp.zeros((slot_total, 9, LANES), jnp.float32).at[slots].set(binned)
    arrived, arrived_labels = (
        lax.all_to_all(
            outgoing.reshape(ranks, capacity, 9, LANES),
            "tm",
            split_axis=0,
            concat_axis=0,
            tiled=True,
        ),
        lax.all_to_all(labels, "tm", split_axis=0, concat_axis=0, tiled=True),
    )
    flat_labels = arrived_labels.reshape(-1)
    targets = flat_labels.astype(jnp.int32)
    targets = jnp.where(targets < 0, owner_tiles, targets)
    solved = combine_maps(arrived.reshape(slot_total, 9, LANES), flat_labels, owner_tiles)
    padded = jnp.concatenate([solved, jnp.zeros((1, 3, LANES), jnp.float32)], axis=0)
    returned = padded[targets].reshape(ranks, capacity, 3, LANES)
    received = lax.all_to_all(returned, "tm", split_axis=0, concat_axis=0, tiled=True)
    own_maps = received.reshape(slot_total, 3, LANES)[slots]
    values_read = read_blocks(own_maps, offsets)
    projected = values_read[:, 0] + cos_blocks * values_read[:, 1] + sin_blocks * values_read[:, 2]
    cleaned = stream - projected.reshape(det_count, samples)
    gathered = jnp.stack(
        [jnp.sum(columns[column] * cleaned, axis=1) for column in range(width_ext)], axis=1
    )
    rims = jnp.concatenate([gathered[:, :2], gathered[:, width_ext - 2 :]], axis=1)
    neighbours = padded_2(rims, (("tm", 1),), 2)
    owned = gathered[:, 2 : width_ext - 2]
    owned = owned.at[:, :2].add(neighbours[:, :2])
    owned = owned.at[:, node_portion - 2 :].add(neighbours[:, 6:])
    image = owned / spacing + BASE_PRIOR * search_vector
    norm_old = lax.psum(jnp.sum(leftover_error * leftover_error), ("tm", "det"))
    curvature = lax.psum(jnp.sum(search_vector * image), ("tm", "det"))
    stride_factor = norm_old / curvature
    fresh_leftover_error = leftover_error - stride_factor * image
    norm_new = lax.psum(jnp.sum(fresh_leftover_error * fresh_leftover_error), ("tm", "det"))
    fresh_offset_coeffs = offset_coeffs + stride_factor * search_vector
    fresh_search_vector = fresh_leftover_error + norm_new / norm_old * search_vector
    return (fresh_offset_coeffs, fresh_leftover_error, fresh_search_vector)


def solution(mesh):
    return jax.shard_map(
        body,
        mesh=mesh,
        in_specs=(
            P("det", "tm"),
            P("det", "tm"),
            P("det", "tm"),
            P("det"),
            P("det", "tm"),
            P("det", "tm"),
            P("det", "tm"),
        ),
        out_specs=(P("det", "tm"), P("det", "tm"), P("det", "tm")),
        check_vma=False,
    )
```

profile of v0, /device:TPU:1, one launch (start us, length us, event | category | flops | bytes accessed | tf_op | source)
XLA Modules:
  0.0 396.8 jit_solution(3352277743797561041)
XLA Ops:
  7.2 2.5 collective-permute-start
  9.7 8.7 %collective-permute-start.1 = (f32[8,2]{0,1:T(2,128)}, f32[8,2]{0,1:T(2,128)S(1)}, u32[]{:S(2)}, u32[]{:S(2)}) collective-permute-start(f32[8,2]{0,1:T(2,128)} %param.21), channel_id=1, source_target_pairs={{2,0},{4,2},{6,4},{8,6},{10,8},{12,10},{14,12},{16,14},{18,16},{20... | collective-permute-start | bytes 200 | tf_op jit(solution)/shard_map/ppermute | solution.py:25
  20.4 1.0 scatter_custom_fusion
  22.1 7.9 %all-to-all-start = ((f32[128,1,2]{2,1,0:T(1,128)}), f32[128,1,2]{2,1,0:T(1,128)S(1)}, u32[]{:S(2)}, u32[]{:S(2)}) async-start(f32[128,1,2]{2,1,0:T(1,128)} %bitcast.8), calls=%async_computation | async-start | bytes 131072 | tf_op jit(solution)/shard_map/all_to_all | solution.py:214
  30.8 1.1 multiply_cosine_fusion
  35.4 2.9 fusion.62
  38.4 1.0 stack.39
  39.4 7.4 %while.26 = (s32[]{:T(128)}, f32[2,64,9,128]{3,2,1,0:T(8,128)S(1)}, f32[2,64,9,128]{3,2,1,0:T(8,128)S(1)}, s32[2,64,128]{2,1,0:T(8,128)S(1)}, s32[]{:T(128)}) while((s32[]{:T(128)}, f32[2,64,9,128]{3,2,1,0:T(8,128)S(1)}, f32[2,64,9,128]{3,2,1,0:T(8,128)S(1)}, s32[2,64,128]{2,1,0:T(8,128)S(1)}, s32[]{:T(128)}) %tuple.87), condition=%wide.region_6.7_spmd.clone, body=%wide.region_5.6_spmd.clone.sunk | while | flops 114294784 | bytes 1147969 | solution.py:102
  39.4 3.7 fusion.69
  43.1 3.7 fusion.69
  46.9 4.3 %scatter_fusion = f32[256,9,128]{2,1,0:T(8,128)S(1)} fusion(f32[256,9,128]{2,1,0:T(8,128)S(1)} %broadcast_in_dim.76, s32[128]{0:T(128)S(1)} %fusion.57, f32[128,9,128]{2,1,0:T(8,128)S(1)} %bitcast.72), kind=kCustom, calls=%fused_computation.3 | custom fusion | bytes 1769984 | tf_op jit(solution)/shard_map/scatter | solution.py:205
  51.3 1.6 copy.29
  52.9 13.2 %all-to-all-start.1 = ((f32[128,2,9,128]{3,1,2,0:T(2,128)}), f32[128,2,9,128]{3,1,2,0:T(2,128)S(1)}, u32[]{:S(2)}, u32[]{:S(2)}) async-start(f32[128,2,9,128]{3,1,2,0:T(2,128)} %copy.29), calls=%async_computation.1 | async-start | bytes 2359296 | tf_op jit(solution)/shard_map/all_to_all | solution.py:207
  66.7 31.4 %all-to-all-done.1 = f32[128,2,9,128]{3,1,2,0:T(2,128)S(1)} async-done(((f32[128,2,9,128]{3,1,2,0:T(2,128)}), f32[128,2,9,128]{3,1,2,0:T(2,128)S(1)}, u32[]{:S(2)}, u32[]{:S(2)}) %all-to-all-start.1) | async-done | bytes 1179680 | tf_op jit(solution)/shard_map/all_to_all | solution.py:207
  99.3 3.5 broadcast_in_dim.73
  102.8 30.1 %scatter_fusion.1 = f32[1025,9,128]{2,1,0:T(8,128)} fusion(f32[1025,9,128]{2,1,0:T(8,128)} %broadcast_in_dim.73, s32[256]{0:T(256)S(1)} %bitcast.80, f32[256,9,128]{2,1,0:T(8,128)S(1)} %copy.31), kind=kCustom, calls=%fused_computation.4 | custom fusion | flops 294912 | bytes 3539968 | tf_op jit(solution)/shard_map/scatter-add | solution.py:76
  133.0 3.9 slice.114
  136.9 3.6 copy.42
  140.5 36.8 %all-reduce.4.cloned.1.call-done = f32[1024,9,128]{2,0,1:T(8,128)} async-done(((f32[1024,9,128]{2,0,1:T(8,128)}), f32[1024,9,128]{2,0,1:T(8,128)}) %all-reduce.4.cloned.1.call-update) | async-done | bytes 4718608 | tf_op jit(solution)/shard_map/psum | solution.py:81
  177.3 2.9 add_divide_fusion.2
  181.7 1.1 copy.43
  183.2 1.0 gather_fusion
  184.2 0.9 copy.35
  185.1 13.8 %all-to-all-start.2 = ((f32[128,2,3,128]{3,1,2,0:T(2,128)}), f32[128,2,3,128]{3,1,2,0:T(2,128)S(1)}, u32[]{:S(2)}, u32[]{:S(2)}) async-start(f32[128,2,3,128]{3,1,2,0:T(2,128)} %copy.35), calls=%async_computation.2 | async-start | bytes 786432 | tf_op jit(solution)/shard_map/all_to_all | solution.py:222
  199.6 15.9 %all-to-all-done.2 = f32[128,2,3,128]{3,1,2,0:T(2,128)S(1)} async-done(((f32[128,2,3,128]{3,1,2,0:T(2,128)}), f32[128,2,3,128]{3,1,2,0:T(2,128)S(1)}, u32[]{:S(2)}, u32[]{:S(2)}) %all-to-all-start.2) | async-done | bytes 393248 | tf_op jit(solution)/shard_map/all_to_all | solution.py:222
  216.7 8.1 %while.27 = (s32[]{:T(128)}, f32[2,64,3,128]{3,2,1,0:T(4,128)S(1)}, f32[2,64,3,128]{3,2,1,0:T(4,128)S(1)}, s32[2,64,128]{2,1,0:T(8,128)S(1)}, s32[]{:T(128)}) while((s32[]{:T(128)}, f32[2,64,3,128]{3,2,1,0:T(4,128)S(1)}, f32[2,64,3,128]{3,2,1,0:T(4,128)S(1)}, s32[2,64,128]{2,1,0:T(8,128)S(1)}, s32[]{:T(128)}) %tuple.96), condition=%wide.region_11.12_spmd.clone, body=%wide.region_10.11_spmd.clone.sunk | while | flops 38797312 | bytes 361537 | solution.py:125
  216.7 4.0 %fusion.71 = f32[2,64,3,128]{3,2,1,0:T(4,128)S(1)} fusion(f32[2,64,3,128]{3,2,1,0:T(4,128)S(1)} %get-tuple-element.259, s32[]{:T(128)} %get-tuple-element.258, s32[64,128]{1,0:T(8,128)S(1)} %dynamic-slice_bitcast_fusion.5, f32[2,64,3,128]{3,2,1,0:T(4,128)S(1)} %get-tuple-element.265), kind=kOutput, calls=%fused_computation.20.clone.1 | convolution fusion | flops 38797312 | bytes 295936 | tf_op jit(solution)/shard_map/while/body/eval_jaxpr/rhe,roe->rho/dot_general | solution.py:121
  220.8 4.0 %fusion.71 = f32[2,64,3,128]{3,2,1,0:T(4,128)S(1)} fusion(f32[2,64,3,128]{3,2,1,0:T(4,128)S(1)} %get-tuple-element.259, s32[]{:T(128)} %get-tuple-element.258, s32[64,128]{1,0:T(8,128)S(1)} %dynamic-slice_bitcast_fusion.5, f32[2,64,3,128]{3,2,1,0:T(4,128)S(1)} %get-tuple-element.265), kind=kOutput, calls=%fused_computation.20.clone.1 | convolution fusion | flops 38797312 | bytes 295936 | tf_op jit(solution)/shard_map/while/body/eval_jaxpr/rhe,roe->rho/dot_general | solution.py:121
  227.1 6.1 %collective-permute-start.3 = (f32[8,2]{0,1:T(2,128)S(1)}, f32[8,2]{0,1:T(2,128)S(1)}, u32[]{:S(2)}, u32[]{:S(2)}) collective-permute-start(f32[8,2]{0,1:T(2,128)S(1)} %pad_maximum_fusion.2), channel_id=1, source_target_pairs={{2,0},{4,2},{6,4},{8,6},{10,8},{12,10},{14,12},{16,14},{18,16},{20... | collective-permute-start | bytes 200 | tf_op jit(solution)/shard_map/ppermute | solution.py:25
  233.2 0.9 collective-permute-done.2
  234.8 77.8 %all-reduce.1 = (f32[]{:T(128)}, f32[]{:T(128)}) all-reduce(f32[]{:T(128)} %multiply_reduce_fusion.8, f32[]{:T(128)} %get-tuple-element.158), channel_id=1, replica_groups=mesh['tm'=128,'det'=2] {'tm','det'}, use_global_device_ids=true, to_apply=%region_1.2 | all-reduce | flops 2 | bytes 16 | tf_op jit(solution)/shard_map/psum | solution.py:236
  314.6 73.5 %psum.31 = f32[]{:T(128)} all-reduce(f32[]{:T(128)} %get-tuple-element.156), channel_id=1, replica_groups=mesh['tm'=128,'det'=2] {'tm','det'}, use_global_device_ids=true, to_apply=%region_21.22 | all-reduce | flops 1 | bytes 8 | tf_op jit(solution)/shard_map/psum | solution.py:240
  (92 shorter events, 16.7 us)
Async XLA Ops:
  7.2 27.2 %collective-permute-start = (f32[8,2]{0,1:T(2,128)}, f32[8,2]{0,1:T(2,128)S(1)}, u32[]{:S(2)}, u32[]{:S(2)}) collective-permute-start(f32[8,2]{0,1:T(2,128)} %param.21), channel_id=1, source_target_pairs={{0,2},{2,4},{4,6},{6,8},{8,10},{10,12},{12,14},{14,16},{16,18},{18... | collective-permute-start | bytes 200 | tf_op jit(solution)/shard_map/ppermute | solution.py:23
  9.7 25.1 %collective-permute-start.1 = (f32[8,2]{0,1:T(2,128)}, f32[8,2]{0,1:T(2,128)S(1)}, u32[]{:S(2)}, u32[]{:S(2)}) collective-permute-start(f32[8,2]{0,1:T(2,128)} %param.21), channel_id=1, source_target_pairs={{2,0},{4,2},{6,4},{8,6},{10,8},{12,10},{14,12},{16,14},{18,16},{20... | collective-permute-start | bytes 200 | tf_op jit(solution)/shard_map/ppermute | solution.py:25
  22.1 30.8 %all-to-all-start = ((f32[128,1,2]{2,1,0:T(1,128)}), f32[128,1,2]{2,1,0:T(1,128)S(1)}, u32[]{:S(2)}, u32[]{:S(2)}) async-start(f32[128,1,2]{2,1,0:T(1,128)} %bitcast.8), calls=%async_computation | async-start | bytes 131072 | tf_op jit(solution)/shard_map/all_to_all | solution.py:214
  52.9 45.2 %all-to-all-start.1 = ((f32[128,2,9,128]{3,1,2,0:T(2,128)}), f32[128,2,9,128]{3,1,2,0:T(2,128)S(1)}, u32[]{:S(2)}, u32[]{:S(2)}) async-start(f32[128,2,9,128]{3,1,2,0:T(2,128)} %copy.29), calls=%async_computation.1 | async-start | bytes 2359296 | tf_op jit(solution)/shard_map/all_to_all | solution.py:207
  66.2 111.1 %all-reduce.4.cloned.1.call-start = ((), (), s32[]{:S(2)}) async-start(), calls=%async_computation.3 | async-start | bytes 9437184 | tf_op jit(solution)/shard_map/psum | solution.py:81
  177.3 3.8 copy-start
  183.2 15.8 %copy-start.4 = (f32[8,2]{0,1:T(2,128)S(1)}, f32[8,2]{0,1:T(2,128)}, u32[]{:S(2)}) copy-start(f32[8,2]{0,1:T(2,128)} %param.20) | copy-start | bytes 196
  185.1 30.3 %all-to-all-start.2 = ((f32[128,2,3,128]{3,1,2,0:T(2,128)}), f32[128,2,3,128]{3,1,2,0:T(2,128)S(1)}, u32[]{:S(2)}, u32[]{:S(2)}) async-start(f32[128,2,3,128]{3,1,2,0:T(2,128)} %copy.35), calls=%async_computation.2 | async-start | bytes 786432 | tf_op jit(solution)/shard_map/all_to_all | solution.py:222
  216.7 8.8 %copy-start.1 = (f32[8,2048]{1,0:T(8,128)S(1)}, f32[8,2048]{1,0:T(8,128)}, u32[]{:S(2)}) copy-start(f32[8,2048]{1,0:T(8,128)} %param.24) | copy-start | bytes 196612
  216.7 8.8 %copy-start.6 = (s32[8]{0:T(128)S(1)}, s32[8]{0:T(128)}, u32[]{:S(2)}) copy-start(s32[8]{0:T(128)} %param.22) | copy-start | bytes 100
  216.7 17.5 %copy-start.2 = (f32[8,2]{0,1:T(2,128)S(1)}, f32[8,2]{0,1:T(2,128)}, u32[]{:S(2)}) copy-start(f32[8,2]{0,1:T(2,128)} %param.21) | copy-start | bytes 196
  216.7 172.7 %copy-start.5 = (f32[8,2]{0,1:T(2,128)S(1)}, f32[8,2]{0,1:T(2,128)}, u32[]{:S(2)}) copy-start(f32[8,2]{0,1:T(2,128)} %param.19) | copy-start | bytes 196
  226.3 7.9 %collective-permute-start.2 = (f32[8,2]{0,1:T(2,128)S(1)}, f32[8,2]{0,1:T(2,128)S(1)}, u32[]{:S(2)}, u32[]{:S(2)}) collective-permute-start(f32[8,2]{0,1:T(2,128)S(1)} %pad_maximum_fusion.1), channel_id=1, source_target_pairs={{0,2},{2,4},{4,6},{6,8},{8,10},{10,12},{12,14},{14,16},{16,18},{18... | collective-permute-start | bytes 200 | tf_op jit(solution)/shard_map/ppermute | solution.py:23
  227.1 7.0 %collective-permute-start.3 = (f32[8,2]{0,1:T(2,128)S(1)}, f32[8,2]{0,1:T(2,128)S(1)}, u32[]{:S(2)}, u32[]{:S(2)}) collective-permute-start(f32[8,2]{0,1:T(2,128)S(1)} %pad_maximum_fusion.2), channel_id=1, source_target_pairs={{2,0},{4,2},{6,4},{8,6},{10,8},{12,10},{14,12},{16,14},{18,16},{20... | collective-permute-start | bytes 200 | tf_op jit(solution)/shard_map/ppermute | solution.py:25
  314.6 75.4 %copy-start.3 = (f32[8,2]{0,1:T(2,128)}, f32[8,2]{0,1:T(2,128)S(1)}, u32[]{:S(2)}) copy-start(f32[8,2]{0,1:T(2,128)S(1)} %get-tuple-element.157) | copy-start | bytes 196
Sparse Core Ops, SparseCore 0:
  140.6 36.6 all-reduce.3
where the time goes:
time: 399 us; the launch traced here: 397 us
  blocking collectives  151 us (38%)
  waiting for transfers between devices  85 us (21%)
  starting transfers between devices  53.3 us (13%)
  other arithmetic  41.5 us (10%)
  local copies, waits for them, and re-layouts  33 us (8%)
  between operations  17.1 us (4%)
  matrix products  15.4 us (4%)
    psum x1, blocking collectives, body(): norm_old = lax.psum(jnp.sum(leftover_error * leftover_error), ('tm', 'det'))  77.8 us
    psum x1, blocking collectives, body(): lax.psum(jnp.sum(fresh_leftover_error * fresh_leftover_error), ('tm', 'de...  73.5 us
    psum x1, waiting for transfers between devices, combine_maps(): totals = lax.psum(partial_value, 'det')  36.8 us
    all_to_all x1, waiting for transfers between devices, body(): lax.all_to_all(outgoing.reshape(ranks, capacity, 9, LANES), 'tm', split_a...  31.4 us
    scatter-add x1, other arithmetic, place_rows(): jnp.zeros((owner_tiles + 1, 9, LANES), jnp.float32).at[targets].add(rows)  30.1 us
    all_to_all x1, waiting for transfers between devices, body(): lax.all_to_all(returned, 'tm', split_axis=0, concat_axis=0, tiled=True)  15.9 us
    ppermute x2, starting transfers between devices, padded_2(): lax.ppermute(head, axis, [((i + 1) % count, i) for i in range(count)])  14.8 us
    all_to_all x1, starting transfers between devices, body(): lax.all_to_all(returned, 'tm', split_axis=0, concat_axis=0, tiled=True)  13.8 us
  transfers between devices with their start and end apart: 8, of which 4 were waited for; matrix products, arithmetic and copies ran while one was open for 7% of the time, Pallas kernels for 0%

commit v1 on v0

v1 whole, which is shorter than its diff:
```python
import jax
import jax.numpy as jnp
from jax import lax
from jax.experimental import pallas as pl
from jax.experimental.pallas import tpu as pltpu
from jax.sharding import PartitionSpec as P

MESH = pl.DeviceIdType.MESH
F32 = jnp.float32
BF16 = jnp.bfloat16
NX, NY, NZ = 4, 4, 8
RANKS = 128
DETS = 8
LANES = 128
SPACING = 1024
MAP_PRIOR = 1.0
BASE_PRIOR = 0.1
OWNER_SHIFT = 10
MSG = 5


def iota(shape, dim):
    return lax.broadcasted_iota(jnp.int32, shape, dim)


def split3(x):
    hi = x.astype(BF16)
    rest = x - hi.astype(F32)
    mid = rest.astype(BF16)
    low = (rest - mid.astype(F32)).astype(BF16)
    return hi, mid, low


def split2(x):
    hi = x.astype(BF16)
    return hi, (x - hi.astype(F32)).astype(BF16)


def dot(a, b):
    return lax.dot_general(a, b, (((1,), (0,)), ((), ())), preferred_element_type=F32)


def dot_nt(a, b):
    return lax.dot_general(a, b, (((1,), (1,)), ((), ())), preferred_element_type=F32)


def exchange_kernel(
    off_ref, seg_ref, cell_ref, phase_ref, p_ref, r_ref, own_ref, par_ref, out_ref, send_sem, recv_sem, pair_sem, local_sem
):
    me = lax.axis_index("tm")
    core = lax.axis_index("det")
    y, x, z = me // (NX * NZ), (me // NZ) % NX, me % NZ

    def target(step):
        t = (step * 37) % RANKS
        ty = (y + t // (NX * NZ)) % NY
        tx = (x + (t // NZ) % NX) % NX
        tz = (z + t % NZ) % NZ
        return (ty * NX + tx) * NZ + tz

    barrier = pltpu.get_barrier_semaphore()

    def greet(step, carry):
        pl.semaphore_signal(barrier, inc=1, device_id={"tm": target(step)}, device_id_type=MESH)
        return carry

    lax.fori_loop(1, RANKS, greet, 0)
    pl.semaphore_signal(barrier, inc=1, device_id={"det": 1 - core}, device_id_type=MESH)

    lane8, sub8 = iota((8, LANES), 1), iota((8, LANES), 0)
    seg = seg_ref[...].astype(F32)
    wide = jnp.zeros((8, LANES), F32)
    for k in range(16):
        wide = jnp.where(lane8 // 8 == k, seg[:, k : k + 1], wide)
    own_lane = lane8 % 8 == sub8
    tile_row = jnp.sum(jnp.where(own_lane, wide, 0.0), axis=0, keepdims=True).astype(jnp.int32)
    owner_row = tile_row >> OWNER_SHIFT
    local_row = ((tile_row & ((1 << OWNER_SHIFT) - 1)) + 1).astype(F32)
    lane1 = iota((1, LANES), 1)
    start_row = (lane1 // 8) * LANES
    for d in range(DETS):
        start_row = jnp.where(lane1 % 8 == d, start_row - off_ref[d], start_row)
    start_row = start_row.astype(F32)
    det_row = (lane1 % 8).astype(F32)

    def placed(values, first):
        shifted = lane8 - first
        both = jnp.where(shifted // 8 == 0, values[:, 0:1], values[:, 1:2])
        keep = (shifted >= 0) & (shifted < 16) & own_lane
        return jnp.sum(jnp.where(keep, both, 0.0), axis=0, keepdims=True)

    vec_row = placed(p_ref[...], 16) + placed(r_ref[...], 32)

    lane, sub = iota((RANKS, LANES), 1), iota((RANKS, LANES), 0)
    lane_f = lane.astype(F32)
    member = owner_row == sub
    first = jnp.min(jnp.where(member, lane_f, 512.0), axis=1, keepdims=True)
    last = jnp.max(jnp.where(member, lane_f, -1.0), axis=1, keepdims=True)
    pick0 = lane_f == first
    pick1 = (lane_f == last) & (last > first)
    one_hot = jnp.concatenate(
        [jnp.where(pick0, 1.0, 0.0), jnp.where(pick1, 1.0, 0.0)], axis=0
    ).astype(BF16)
    cells = jnp.concatenate(
        [cell_ref[:, k * LANES : (k + 1) * LANES] for k in range(16)], axis=0
    ).astype(F32).astype(BF16)
    phases = jnp.concatenate([phase_ref[:, k * LANES : (k + 1) * LANES] for k in range(16)], axis=0)
    rows = dot(one_hot, jnp.concatenate([cells, *split3(phases)], axis=1))
    phase_rows = rows[:, 128:256] + rows[:, 256:384] + rows[:, 384:512]
    meta = jnp.where(lane >= 16, vec_row, 0.0)
    column = 0
    for row in (local_row, start_row, det_row):
        for pick in (pick0, pick1):
            value = jnp.sum(jnp.where(pick, row, 0.0), axis=1, keepdims=True)
            meta = jnp.where(lane == column, value, meta)
            column += 1
    out_ref[:, 0, :] = rows[:RANKS, :128]
    out_ref[:, 1, :] = rows[RANKS:, :128]
    out_ref[:, 2, :] = phase_rows[:RANKS]
    out_ref[:, 3, :] = phase_rows[RANKS:]
    out_ref[:, 4, :] = meta

    mine = pltpu.make_async_copy(out_ref.at[me], own_ref.at[me], local_sem)
    mine.start()
    pl.semaphore_wait(barrier, RANKS)

    def send(step, carry):
        dst = target(step)
        pltpu.make_async_remote_copy(
            src_ref=out_ref.at[dst],
            dst_ref=own_ref.at[me],
            send_sem=send_sem,
            recv_sem=recv_sem,
            device_id={"tm": dst},
            device_id_type=MESH,
        ).start()
        return carry

    lax.fori_loop(1, RANKS, send, 0)
    mine.wait()
    rest = pltpu.make_async_remote_copy(
        src_ref=out_ref.at[pl.ds(0, RANKS - 1)],
        dst_ref=own_ref.at[pl.ds(0, RANKS - 1)],
        send_sem=send_sem,
        recv_sem=recv_sem,
        device_id={"tm": me},
        device_id_type=MESH,
    )
    rest.wait_recv()
    pair = pltpu.make_async_remote_copy(
        src_ref=own_ref,
        dst_ref=par_ref,
        send_sem=pair_sem.at[0],
        recv_sem=pair_sem.at[1],
        device_id={"det": 1 - core},
        device_id_type=MESH,
    )
    pair.start()
    rest.wait_send()
    pair.wait()


def cos_sin(phase):
    angle = 2.0 * phase
    quarter = jnp.floor(angle * 0.6366197723675814 + 0.5)
    r = angle - quarter * 1.5703125
    r = r - quarter * 4.837512969970703125e-4
    r = r - quarter * 7.54978995489188216e-8
    q = quarter.astype(jnp.int32) & 3
    sq = r * r
    sine = r + r * sq * (-1.6666654611e-1 + sq * (8.3321608736e-3 + sq * -1.9515295891e-4))
    cosine = 1.0 - 0.5 * sq + sq * sq * (
        4.166664568298827e-2 + sq * (-1.388731625493765e-3 + sq * 2.443315711809948e-5)
    )
    odd = (q & 1) == 1
    big_c = jnp.where(odd, sine, cosine)
    big_s = jnp.where(odd, cosine, sine)
    big_c = jnp.where((q == 1) | (q == 2), -big_c, big_c)
    big_s = jnp.where(q >= 2, -big_s, big_s)
    return big_c, big_s


def spline_weights(fraction):
    square = fraction * fraction
    cube = square * fraction
    rest = 1.0 - fraction
    sixth = 1.0 / 6.0
    return (
        rest * rest * rest * sixth,
        (3.0 * cube - 6.0 * square + 4.0) * sixth,
        (-3.0 * cube + 3.0 * square + 3.0 * fraction + 1.0) * sixth,
        cube * sixth,
    )


def solve_pixels(sums):
    total, s_cos, s_sin, hits, cos_sum, sin_sum, cos_cos, cos_sin_, sin_sin = sums
    si = hits + MAP_PRIOR
    sq = cos_cos + MAP_PRIOR
    su = sin_sin + MAP_PRIOR
    m1 = sq * su - cos_sin_ * cos_sin_
    m2 = sin_sum * cos_sin_ - cos_sum * su
    m3 = cos_sum * cos_sin_ - sin_sum * sq
    m4 = si * su - sin_sum * sin_sum
    m5 = cos_sum * sin_sum - si * cos_sin_
    m6 = si * sq - cos_sum * cos_sum
    inverse = 1.0 / (si * m1 + cos_sum * m2 + sin_sum * m3)
    return (
        (m1 * total + m2 * s_cos + m3 * s_sin) * inverse,
        (m2 * total + m4 * s_cos + m5 * s_sin) * inverse,
        (m3 * total + m5 * s_cos + m6 * s_sin) * inverse,
    )


SUB = 64
GROUP = 8
META_I, META_G, META_S = 80, 81, 82


def owner_kernel(
    own_ref, par_ref, out_ref, d_ref, cell_ref, phase_ref, meta_ref, row_ref, x_ref, b_ref, bs_ref, t_ref, stream_ref, c_ref, s_ref, v_ref, img_ref
):
    core = lax.axis_index("det")
    lane, sub = iota((RANKS, LANES), 1), iota((RANKS, LANES), 0)
    sub_f = sub.astype(F32)
    upper = jnp.where(sub < lane, 1.0, 0.0).astype(BF16)
    metas, turned = [], []
    for ref in (own_ref, par_ref):
        metas.append(ref[:, 4, :])
        turned.append(metas[-1].T)
    rows4 = jnp.concatenate([turned[0][0:2], turned[1][0:2], jnp.zeros((4, LANES), F32)], axis=0)
    tiles4 = rows4.astype(jnp.int32)
    mine4 = jnp.where((tiles4 > 0) & (((tiles4 - 1) & 1) == core), 1.0, 0.0)
    inside = dot(mine4.astype(BF16), upper)
    totals = jnp.sum(mine4, axis=1, keepdims=True)
    ranks = []
    base = jnp.zeros((1, 1), F32)
    for g in range(4):
        ranks.append(jnp.where(mine4[g : g + 1] > 0.0, inside[g : g + 1] + base, -1.0))
        base = base + totals[g : g + 1]
    count = jnp.sum(mine4).astype(jnp.int32)
    chunks = (count + 127) // 128
    subs = (count + SUB - 1) // SUB
    wides = (count + 255) // 256

    for b, ref in enumerate((own_ref, par_ref)):
        meta = jnp.where(lane < 48, metas[b], 0.0)
        p_only = jnp.where((lane >= 16) & (lane < 32), meta, 0.0)
        meta = meta + pltpu.roll(pltpu.roll(p_only, 1, 0), 32, 1)
        meta = meta + pltpu.roll(pltpu.roll(p_only, RANKS - 1, 0), 48, 1)
        meta = jnp.where(lane == META_I, sub_f, meta)
        group = (core if b == 0 else 1 - core) * 8
        meta = jnp.where(lane == META_G, group.astype(F32), meta)
        for s in range(2):
            at = pl.ds((2 * b + s) * 128, 128)
            d_ref[at, 0:128] = ref[:, s, :].astype(BF16)
            for k, part in enumerate(split3(ref[:, 2 + s, :])):
                d_ref[at, (1 + k) * 128 : (2 + k) * 128] = part
            tagged = jnp.where(lane == META_S, float(s), meta)
            for k, part in enumerate(split3(tagged)):
                d_ref[at, (4 + k) * 128 : (5 + k) * 128] = part

    def compact(i, carry):
        want = sub_f + (i * 128).astype(F32)
        pick = jnp.concatenate(
            [jnp.where(ranks[g] == want, 1.0, 0.0).astype(BF16) for g in range(4)], axis=1
        )
        got = dot(pick, d_ref[...])
        at = pl.ds(pl.multiple_of(i * 128, 128), 128)
        cell_ref[at, :] = got[:, 0:128]
        phase_ref[at, :] = got[:, 128:256] + got[:, 256:384] + got[:, 384:512]
        meta = got[:, 512:640] + got[:, 640:768] + got[:, 768:896]
        second = meta[:, META_S : META_S + 1] > 0.5
        for column in range(3):
            value = jnp.where(
                second, meta[:, 2 * column + 1 : 2 * column + 2], meta[:, 2 * column : 2 * column + 1]
            )
            meta = jnp.where(lane == column, value, meta)
        meta_ref[at, :] = meta
        flat = meta.T
        row_ref[i, 0:1, :] = flat[0:1]
        row_ref[i, 1:2, :] = flat[META_I : META_I + 1]
        return carry

    row_ref[...] = jnp.full(row_ref.shape, -1.0, F32)
    lax.fori_loop(0, chunks, compact, 0)

    lane_s = iota((SUB, LANES), 1)
    lane_sf = lane_s.astype(F32)

    def places(meta):
        u = meta[:, 1:2] + lane_sf
        interval = jnp.floor(u * (1.0 / SPACING))
        fraction = (u - interval * SPACING) * (1.0 / SPACING)
        return interval, spline_weights(fraction)

    def prepare(i, carry):
        at = pl.ds(pl.multiple_of(i * SUB, SUB), SUB)
        meta = meta_ref[at, :]
        interval, weights = places(meta)
        det = meta[:, 2:3].astype(jnp.int32)
        hit = (lane_s & 7) == det
        knots = []
        for start in (48, 56, 16, 24, 64, 72):
            keep = hit & (lane_s >= start) & (lane_s < start + 8)
            knots.append(jnp.sum(jnp.where(keep, meta, 0.0), axis=1, keepdims=True))
        early, late = interval < -0.5, interval > 0.5
        stream = jnp.zeros((SUB, LANES), F32)
        for k in range(4):
            knot = jnp.where(early, knots[k], jnp.where(late, knots[k + 2], knots[k + 1]))
            stream = stream + weights[k] * knot
        c, s = cos_sin(phase_ref[at, :])
        stream_ref[at, :] = stream
        c_ref[at, :] = c
        s_ref[at, :] = s
        channels = (stream, stream * c, stream * s, jnp.ones_like(c), c, s, c * c, c * s, s * s)
        for ch, value in enumerate(channels):
            x_ref[pl.ds(i * SUB * 16 + ch, SUB, stride=16), :] = value
        return carry

    lax.fori_loop(0, subs, prepare, 0)

    def bin_group(i, carry):
        cells = cell_ref[pl.ds(pl.multiple_of(i * GROUP, GROUP), GROUP), :]
        for j in range(GROUP):
            hot = jnp.where(cells[j : j + 1, :] == sub_f, 1.0, 0.0).astype(BF16)
            at = pl.ds(pl.multiple_of((i * GROUP + j) * 16, 16), 16)
            hi, low = split2(x_ref[at, :])
            both = dot_nt(jnp.concatenate([hi, low], axis=0), hot)
            b_ref[at, :] = both[0:16] + both[16:32]
        return carry

    groups = (count + GROUP - 1) // GROUP
    lax.fori_loop(0, groups, bin_group, 0)

    def spread(i, carry):
        live = (iota((SUB, LANES), 0) + i * SUB) < groups * GROUP
        low_at = (i // 4) * 512 + (i % 4) * SUB
        for ch in range(9):
            value = b_ref[pl.ds(i * SUB * 16 + ch, SUB, stride=16), :]
            hi, low = split2(jnp.where(live, value, 0.0))
            cols = slice(ch * 128, (ch + 1) * 128)
            bs_ref[pl.ds(pl.multiple_of(low_at, SUB), SUB), cols] = hi
            bs_ref[pl.ds(pl.multiple_of(low_at + 256, SUB), SUB), cols] = low
        return carry

    lax.fori_loop(0, wides * 4, spread, 0)

    def merge(i, carry):
        at = pl.ds(pl.multiple_of(i * 128, 128), 128)
        tile_column = meta_ref[at, 0:1]

        def part(k):
            same = [
                jnp.where(tile_column == row_ref[2 * k + n, 0:1, :], 1.0, 0.0).astype(BF16) for n in range(2)
            ]
            same = jnp.concatenate(same + same, axis=1)
            return dot(same, bs_ref[pl.ds(pl.multiple_of(k * 512, 512), 512), :])

        t_ref[at, :] = part(0)

        @pl.when(wides > 1)
        def _():
            t_ref[at, :] += part(1)

        return carry

    lax.fori_loop(0, chunks, merge, 0)

    def finish(i, carry):
        at = pl.ds(pl.multiple_of(i * SUB, SUB), SUB)
        maps = solve_pixels(tuple(t_ref[at, ch * 128 : (ch + 1) * 128] for ch in range(9)))
        index = cell_ref[at, :].astype(jnp.int32)
        read = [jnp.take_along_axis(value, index, axis=1) for value in maps]
        cleaned = stream_ref[at, :] - (read[0] + c_ref[at, :] * read[1] + s_ref[at, :] * read[2])
        meta = meta_ref[at, :]
        interval, weights = places(meta)
        terms = [weight * cleaned for weight in weights]
        detector = (meta[:, 2:3] + meta[:, META_G : META_G + 1]).astype(jnp.int32)
        out = jnp.zeros((SUB, LANES), F32)
        for column in range(6):
            value = jnp.zeros((SUB, LANES), F32)
            for k in range(4):
                m = column - 1 - k
                if -1 <= m <= 1:
                    value = value + jnp.where(interval == float(m), terms[k], 0.0)
            out = jnp.where(lane_s == detector + column * 16, jnp.sum(value, axis=1, keepdims=True), out)
        for k, part in enumerate(split3(out)):
            v_ref[pl.ds(pl.multiple_of(k * 512 + i * SUB, SUB), SUB), :] = part
        return carry

    lax.fori_loop(0, subs, finish, 0)

    def blank(i, carry):
        for k in range(3):
            v_ref[pl.ds(pl.multiple_of(k * 512 + i * SUB, SUB), SUB), :] = jnp.zeros((SUB, LANES), BF16)
        return carry

    lax.fori_loop(subs, chunks * 2, blank, 0)
    img_ref[...] = jnp.zeros_like(img_ref)

    def gather_image(i, carry):
        hot = jnp.where(row_ref[i, 1:2, :] == sub_f, 1.0, 0.0).astype(BF16)
        for k in range(3):
            img_ref[...] += dot(hot, v_ref[pl.ds(pl.multiple_of(k * 512 + i * 128, 128), 128), :])
        return carry

    lax.fori_loop(0, chunks, gather_image, 0)
    image = img_ref[...].T
    for g in range(2):
        for n in range(2):
            def rows(c):
                return image[c * 16 + g * 8 : c * 16 + g * 8 + 8]
            value = rows(2 + n) + pltpu.roll(rows(n), RANKS - 1, 1) + pltpu.roll(rows(4 + n), 1, 1)
            out_ref[0, g * 16 + n * 8 : g * 16 + n * 8 + 8, :] = value
    for k in range(2):
        own = turned[0][16 + 16 * k : 32 + 16 * k]
        par = turned[1][16 + 16 * k : 32 + 16 * k]
        out_ref[1 + k, 0:16, :] = jnp.where(core == 0, own, par)
        out_ref[1 + k, 16:32, :] = jnp.where(core == 0, par, own)


def reduce_kernel(
    in_ref, x_in, r_in, p_in, x_out, r_out, p_out, first_ref, hold_ref, z_ref, y_ref, x_ref, full_ref, send_sem, recv_sem
):
    me = lax.axis_index("tm")
    core = lax.axis_index("det")
    y, x, z = me // (NX * NZ), (me // NZ) % NX, me % NZ
    barrier = pltpu.get_barrier_semaphore()
    dims = (
        (NZ, z, lambda k: me - z + k, z_ref),
        (NY, y, lambda k: me + (k - y) * (NX * NZ), y_ref),
        (NX, x, lambda k: me + (k - x) * NZ, x_ref),
    )
    pl.semaphore_signal(barrier, inc=1, device_id={"det": 1 - core}, device_id_type=MESH)
    for size, at, peer, _ in dims:
        for step in range(1, size):
            pl.semaphore_signal(
                barrier, inc=1, device_id={"tm": peer((at + step) % size)}, device_id_type=MESH
            )
    pl.semaphore_wait(barrier, 1 + (NZ - 1) + (NY - 1) + (NX - 1))

    mine = pl.ds(pl.multiple_of(core * 16, 16), 16)
    other = pl.ds(pl.multiple_of((1 - core) * 16, 16), 16)
    pair = pltpu.make_async_remote_copy(
        src_ref=in_ref.at[0, other],
        dst_ref=first_ref,
        send_sem=send_sem.at[0],
        recv_sem=recv_sem.at[0],
        device_id={"det": 1 - core},
        device_id_type=MESH,
    )
    pair.start()
    pair.wait()
    total = in_ref[0, mine, :] + first_ref[...]
    for stage, (size, at, peer, buf) in enumerate(dims):
        hold_ref[stage] = total
        buf[at] = total
        copies = []
        for step in range(1, size):
            copy = pltpu.make_async_remote_copy(
                src_ref=hold_ref.at[stage],
                dst_ref=buf.at[at],
                send_sem=send_sem.at[1 + stage],
                recv_sem=recv_sem.at[1 + stage],
                device_id={"tm": peer((at + step) % size)},
                device_id_type=MESH,
            )
            copy.start()
        rest = pltpu.make_async_remote_copy(
            src_ref=buf.at[pl.ds(0, size - 1)],
            dst_ref=buf.at[pl.ds(0, size - 1)],
            send_sem=send_sem.at[1 + stage],
            recv_sem=recv_sem.at[1 + stage],
            device_id={"tm": me},
            device_id_type=MESH,
        )
        rest.wait_recv()
        rest.wait_send()
        total = buf[0]
        for k in range(1, size):
            total = total + buf[k]
    hold_ref[3] = total
    full_ref[mine, :] = total
    last = pltpu.make_async_remote_copy(
        src_ref=hold_ref.at[3],
        dst_ref=full_ref.at[mine],
        send_sem=send_sem.at[4],
        recv_sem=recv_sem.at[4],
        device_id={"det": 1 - core},
        device_id_type=MESH,
    )
    last.start()
    last.wait()

    p, r = in_ref[1], in_ref[2]
    image = full_ref[...] * (1.0 / SPACING) + BASE_PRIOR * p

    def total_of(value):
        return jnp.sum(jnp.sum(value, axis=1, keepdims=True), axis=0, keepdims=True)

    norm_old = total_of(r * r)
    alpha = norm_old / total_of(p * image)
    fresh = r - alpha * image
    beta = total_of(fresh * fresh) / norm_old
    here = jnp.sum(jnp.where(iota((32, LANES), 1) == me, image, 0.0), axis=1, keepdims=True)
    half = jnp.where(core == 0, here[0:16], here[16:32])
    local = jnp.where(iota((8, 2), 1) == 0, half[0:8], half[8:16])
    p_own = p_in[...]
    fresh_own = r_in[...] - alpha * local
    x_out[...] = x_in[...] + alpha * p_own
    r_out[...] = fresh_own
    p_out[...] = fresh_own + beta * p_own


def vmem():
    return pl.BlockSpec(memory_space=pltpu.VMEM)


def body(offsets, residual, search, lattice, cells, phases, tiles):
    message = jax.ShapeDtypeStruct((RANKS, MSG, LANES), F32)
    own, par = pl.pallas_call(
        exchange_kernel,
        out_shape=(message, message),
        in_specs=[pl.BlockSpec(memory_space=pltpu.SMEM)] + [vmem()] * 5,
        out_specs=(vmem(), vmem()),
        scratch_shapes=[
            pltpu.VMEM((RANKS, MSG, LANES), F32),
            pltpu.SemaphoreType.DMA,
            pltpu.SemaphoreType.DMA,
            pltpu.SemaphoreType.DMA((2,)),
            pltpu.SemaphoreType.DMA,
        ],
        compiler_params=pltpu.CompilerParams(collective_id=0, has_side_effects=True),
        name="exchange",
    )(lattice, tiles, cells, phases, search, residual)
    parts = pl.pallas_call(
        owner_kernel,
        out_shape=jax.ShapeDtypeStruct((3, 32, LANES), F32),
        in_specs=[vmem()] * 2,
        out_specs=vmem(),
        scratch_shapes=[
            pltpu.VMEM((512, 896), BF16),
            pltpu.VMEM((512, LANES), F32),
            pltpu.VMEM((512, LANES), F32),
            pltpu.VMEM((512, LANES), F32),
            pltpu.VMEM((4, 8, LANES), F32),
            pltpu.VMEM((512 * 16, LANES), F32),
            pltpu.VMEM((512 * 16, LANES), F32),
            pltpu.VMEM((1024, 9 * LANES), BF16),
            pltpu.VMEM((512, 9 * LANES), F32),
            pltpu.VMEM((512, LANES), F32),
            pltpu.VMEM((512, LANES), F32),
            pltpu.VMEM((512, LANES), F32),
            pltpu.VMEM((3 * 512, LANES), BF16),
            pltpu.VMEM((RANKS, LANES), F32),
        ],
        name="owner",
    )(own, par)
    small = jax.ShapeDtypeStruct((DETS, 2), F32)
    return pl.pallas_call(
        reduce_kernel,
        out_shape=(small, small, small),
        in_specs=[vmem()] * 4,
        out_specs=(vmem(),) * 3,
        scratch_shapes=[
            pltpu.VMEM((16, LANES), F32),
            pltpu.VMEM((4, 16, LANES), F32),
            pltpu.VMEM((NZ, 16, LANES), F32),
            pltpu.VMEM((NY, 16, LANES), F32),
            pltpu.VMEM((NX, 16, LANES), F32),
            pltpu.VMEM((32, LANES), F32),
            pltpu.SemaphoreType.DMA((5,)),
            pltpu.SemaphoreType.DMA((5,)),
        ],
        compiler_params=pltpu.CompilerParams(collective_id=1, has_side_effects=True),
        name="reduce",
    )(parts, offsets, residual, search)


def solution(mesh):
    return jax.shard_map(
        body,
        mesh=mesh,
        in_specs=(
            P("det", "tm"),
            P("det", "tm"),
            P("det", "tm"),
            P("det"),
            P("det", "tm"),
            P("det", "tm"),
            P("det", "tm"),
        ),
        out_specs=(P("det", "tm"), P("det", "tm"), P("det", "tm")),
        check_vma=False,
    )
```

time: 399 us -> 70.4 us (0.18)
  blocking collectives: 151 us -> 0 us
  waiting for transfers between devices: 85 us -> 0 us
  Pallas kernels: 0 us -> 64.1 us
  starting transfers between devices: 53.3 us -> 0 us
  other arithmetic: 41.5 us -> 0 us
  local copies, waits for them, and re-layouts: 33 us -> 5.34 us
  between operations: 17.1 us -> 0.68 us
  matrix products: 15.4 us -> 0 us
    psum x2 -> x0, blocking collectives: 151 us -> none  [the longest x1 77.8 us: body(): norm_old = lax.psum(jnp.sum(leftover_error * leftover_error), ('tm', 'det'))]
    pallas_call x0 -> x3, Pallas kernels: none -> 64.1 us  [the longest x1 31.2 us: body(): pl.pallas_call(exchange_kernel, out_shape=(message, message), in_specs=[p...]
    all_to_all x3 -> x0, waiting for transfers between devices: 47.3 us -> none  [the longest x1 31.4 us: body(): lax.all_to_all(outgoing.reshape(ranks, capacity, 9, LANES), 'tm', split_a...]
    psum x1 -> x0, waiting for transfers between devices: 36.8 us -> none  [combine_maps(): totals = lax.psum(partial_value, 'det')]
    all_to_all x3 -> x0, starting transfers between devices: 34.9 us -> none  [the longest x1 13.8 us: body(): lax.all_to_all(returned, 'tm', split_axis=0, concat_axis=0, tiled=True)]
    scatter-add x1 -> x0, other arithmetic: 30.1 us -> none  [place_rows(): jnp.zeros((owner_tiles + 1, 9, LANES), jnp.float32).at[targets].add(rows)]
    ppermute x4 -> x0, starting transfers between devices: 18.2 us -> none  [the longest x2 14.8 us: padded_2(): lax.ppermute(head, axis, [((i + 1) % count, i) for i in range(count)])]
    dot_general x4 -> x0, matrix products: 15.4 us -> none  [the longest x2 8.09 us: read_one_group(): jnp.einsum('rhe,roe->rho', input_arrays[0], indicator_matrix, precision=l...]
  transfers between devices with their start and end apart: 8 -> 0, of which waited for: 4 -> 0; matrix products, arithmetic and copies ran while one was open for 7% -> 0% of each run, Pallas kernels for 0% -> 0%
where the time goes in v1:
time: 70.4 us; the launch traced here: 70.1 us
  Pallas kernels  64.1 us (91%)
  local copies, waits for them, and re-layouts  5.34 us (8%)
    pallas_call x1, Pallas kernels, body(): pl.pallas_call(exchange_kernel, out_shape=(message, message), in_specs=[p...  31.2 us
    pallas_call x1, Pallas kernels, body(): pl.pallas_call(reduce_kernel, out_shape=(small, small, small), in_specs=[...  21.6 us
    pallas_call x1, Pallas kernels, body(): pl.pallas_call(owner_kernel, out_shape=jax.ShapeDtypeStruct((3, 32, LANES...  11.3 us
    unnamed x11, local copies, waits for them, and re-layouts  2.75 us
    pallas_call x3, local copies, waits for them, and re-layouts, body(): pl.pallas_call(reduce_kernel, out_shape=(small, small, small), in_specs=[...  2.59 us

profile of v1, /device:TPU:1, one launch (start us, length us, event | category | flops | bytes accessed | tf_op | source)
XLA Modules:
  0.0 70.1 jit_solution(5223435228701177387)
XLA Ops:
  0.6 0.0 copy-start.2
  0.6 1.3 %copy.10.p_ref.p_in = f32[8,2]{1,0:T(8,128)} copy(f32[8,2]{0,1:T(2,128)} %param.9) | data formatting | bytes 128 | tf_op args[2]
  2.0 0.0 copy-done.2
  2.0 0.7 copy.11.r_ref.r_in
  2.7 31.2 %exchange.1 = (f32[128,5,128]{2,1,0:T(8,128)}, f32[128,5,128]{2,1,0:T(8,128)}) custom-call(s32[8]{0:T(128)} %off_ref.1, s32[8,16]{1,0:T(8,128)} %seg_ref.1, s32[8,2048]{1,0:T(8,128)} %cell_ref.1, f32[8,2048]{1,0:T(8,128)} %phase_ref.1, f32[8,2]{1,0:T(8,128)} %copy.10.p_ref.p_in, f32[8,2]{1,0:T(8,128)} %copy.11.r_ref.r_in), custom_call_target="tpu_custom_call" | custom-call | tf_op jit(solution)/shard_map/exchange/pallas_call | solution.py:522
  33.9 0.0 copy-start.3
  33.9 11.3 %owner.1.in_ref = f32[3,32,128]{2,1,0:T(8,128)} custom-call(f32[128,5,128]{2,1,0:T(8,128)} %get-tuple-element.5.own_ref, f32[128,5,128]{2,1,0:T(8,128)} %get-tuple-element.6.par_ref), custom_call_target="tpu_custom_call" | custom-call | tf_op jit(solution)/shard_map/owner/pallas_call | solution.py:537
  45.2 0.0 copy-done.3
  45.2 0.7 copy.12.x_in
  45.8 21.6 %reduce.1 = (f32[8,2]{1,0:T(8,128)}, f32[8,2]{1,0:T(8,128)}, f32[8,2]{1,0:T(8,128)}) custom-call(f32[3,32,128]{2,1,0:T(8,128)} %owner.1.in_ref, f32[8,2]{1,0:T(8,128)} %copy.12.x_in, f32[8,2]{1,0:T(8,128)} %copy.11.r_ref.r_in, f32[8,2]{1,0:T(8,128)} %copy.10.p_ref.p_in), custom_call_target="tpu_custom_call" | custom-call | tf_op jit(solution)/shard_map/reduce/pallas_call | solution.py:561
  67.5 0.0 copy-start.1
  67.5 1.3 %copy.15 = f32[8,2]{0,1:T(2,128)} copy(f32[8,2]{1,0:T(8,128)} %get-tuple-element.7) | data formatting | bytes 128 | tf_op jit(solution)/shard_map/reduce/pallas_call | solution.py:561
  68.8 0.0 copy-start
  68.8 0.0 copy-done.1
  68.8 0.6 copy.16
  69.5 0.0 copy-done
  69.5 0.6 copy.17
Async XLA Ops:
  0.6 1.4 %copy-start.2 = (f32[8,2]{0,1:T(2,128)S(1)}, f32[8,2]{0,1:T(2,128)}, u32[]{:S(2)}) copy-start(f32[8,2]{0,1:T(2,128)} %param.8) | copy-start | bytes 196
  33.9 11.3 %copy-start.3 = (f32[8,2]{0,1:T(2,128)S(1)}, f32[8,2]{0,1:T(2,128)}, u32[]{:S(2)}) copy-start(f32[8,2]{0,1:T(2,128)} %param.7) | copy-start | bytes 196
  67.5 1.3 %copy-start.1 = (f32[8,2]{1,0:T(8,128)S(1)}, f32[8,2]{1,0:T(8,128)}, u32[]{:S(2)}) copy-start(f32[8,2]{1,0:T(8,128)} %get-tuple-element.8) | copy-start | bytes 196
  68.8 0.7 copy-start

commit v2 on v0

v2 whole, which is shorter than its diff:
```python
import jax
import jax.numpy as jnp
from jax import lax
from jax.experimental import pallas as pl
from jax.experimental.pallas import tpu as pltpu
from jax.sharding import PartitionSpec as P

MESH = pl.DeviceIdType.MESH
F32 = jnp.float32
BF16 = jnp.bfloat16
NX, NY, NZ = 4, 4, 8
RANKS = 128
DETS = 8
LANES = 128
SPACING = 1024
MAP_PRIOR = 1.0
BASE_PRIOR = 0.1
OWNER_SHIFT = 10
MSG = 5
PITCH = 8


def iota(shape, dim):
    return lax.broadcasted_iota(jnp.int32, shape, dim)


def split3(x):
    hi = x.astype(BF16)
    rest = x - hi.astype(F32)
    mid = rest.astype(BF16)
    low = (rest - mid.astype(F32)).astype(BF16)
    return hi, mid, low


def split2(x):
    hi = x.astype(BF16)
    return hi, (x - hi.astype(F32)).astype(BF16)


def dot(a, b):
    return lax.dot_general(a, b, (((1,), (0,)), ((), ())), preferred_element_type=F32)


def dot_nt(a, b):
    return lax.dot_general(a, b, (((1,), (1,)), ((), ())), preferred_element_type=F32)


def cos_sin(phase):
    angle = 2.0 * phase
    quarter = jnp.floor(angle * 0.6366197723675814 + 0.5)
    r = angle - quarter * 1.5703125
    r = r - quarter * 4.837512969970703125e-4
    r = r - quarter * 7.54978995489188216e-8
    q = quarter.astype(jnp.int32) & 3
    sq = r * r
    sine = r + r * sq * (-1.6666654611e-1 + sq * (8.3321608736e-3 + sq * -1.9515295891e-4))
    cosine = 1.0 - 0.5 * sq + sq * sq * (
        4.166664568298827e-2 + sq * (-1.388731625493765e-3 + sq * 2.443315711809948e-5)
    )
    odd = (q & 1) == 1
    big_c = jnp.where(odd, sine, cosine)
    big_s = jnp.where(odd, cosine, sine)
    big_c = jnp.where((q == 1) | (q == 2), -big_c, big_c)
    big_s = jnp.where(q >= 2, -big_s, big_s)
    return big_c, big_s


def spline_weights(fraction):
    square = fraction * fraction
    cube = square * fraction
    rest = 1.0 - fraction
    sixth = 1.0 / 6.0
    return (
        rest * rest * rest * sixth,
        (3.0 * cube - 6.0 * square + 4.0) * sixth,
        (-3.0 * cube + 3.0 * square + 3.0 * fraction + 1.0) * sixth,
        cube * sixth,
    )


def solve_pixels(sums):
    total, s_cos, s_sin, hits, cos_sum, sin_sum, cos_cos, cos_sin_, sin_sin = sums
    si = hits + MAP_PRIOR
    sq = cos_cos + MAP_PRIOR
    su = sin_sin + MAP_PRIOR
    m1 = sq * su - cos_sin_ * cos_sin_
    m2 = sin_sum * cos_sin_ - cos_sum * su
    m3 = cos_sum * cos_sin_ - sin_sum * sq
    m4 = si * su - sin_sum * sin_sum
    m5 = cos_sum * sin_sum - si * cos_sin_
    m6 = si * sq - cos_sum * cos_sum
    inverse = 1.0 / (si * m1 + cos_sum * m2 + sin_sum * m3)
    return (
        (m1 * total + m2 * s_cos + m3 * s_sin) * inverse,
        (m2 * total + m4 * s_cos + m5 * s_sin) * inverse,
        (m3 * total + m5 * s_cos + m6 * s_sin) * inverse,
    )


COUNT = 2 * RANKS
BLOCK = 16
GROUPS = RANKS // BLOCK
SUB = 64
META_E, META_P, META_R = 16, 32, 48
LEVELS = ((NZ, 1), (NY, NX * NZ), (NX, NZ))


def near(k, size):
    return jnp.where(k % 2 == 1, (k + 1) // 2, (size - k // 2) % size)


def near_static(k, size):
    return (k + 1) // 2 if k % 2 == 1 else (size - k // 2) % size


def destripe_kernel(
    off_ref, seg_hbm, cell_hbm, phase_hbm, p_hbm, r_hbm, o_hbm, x_out, r_out, p_out, seg_ref, cell_ref, phase_ref, p_ref, r_ref, off_in_ref, halo_ref, out_ref, own_ref, par_ref, x_ref, b_ref, bs_ref, t_ref, stream_ref, c_ref, s_ref, v_ref, part_ref, first_ref, hold_ref, lz_ref, ly_ref, lx_ref, full_ref, in_sem, halo_sem, send_sem, recv_sem, pair_send, pair_recv, red_send, red_recv
):
    me = lax.axis_index("tm")
    core = lax.axis_index("det")
    y, x, z = me // (NX * NZ), (me // NZ) % NX, me % NZ

    def steps(s):
        return near((s % 4), NY), near((s // 4) % 4, NX), near(s // 16, NZ)

    planes = [
        (((y + near_static(k % 4, NY)) % NY) * NX + (x + near_static(k // 4, NX)) % NX) * NZ for k in range(BLOCK)
    ]

    def each_target(act, level):
        depth = (z + near(level, NZ)) % NZ

        def run(first):
            for k in range(first, BLOCK):
                act(level * BLOCK + k, planes[k] + depth, level)

        return run

    barrier = pltpu.get_barrier_semaphore()

    def greet(slot, dst, level):
        pl.semaphore_signal(barrier, inc=1, device_id={"tm": dst}, device_id_type=MESH)

    def greet_level(k, carry):
        each_target(greet, GROUPS - k)(0)
        return carry

    lax.fori_loop(1, GROUPS, greet_level, 0)
    each_target(greet, 0)(1)
    pl.semaphore_signal(barrier, inc=1, device_id={"det": 1 - core}, device_id_type=MESH)

    loads = [
        pltpu.make_async_copy(a, b, in_sem.at[k])
        for k, (a, b) in enumerate(
            ((seg_hbm, seg_ref), (p_hbm, p_ref), (r_hbm, r_ref), (o_hbm, off_in_ref), (cell_hbm, cell_ref), (phase_hbm, phase_ref))
        )
    ]
    for load in loads:
        load.start()
    for load in loads:
        load.wait()

    lane8, sub8 = iota((8, LANES), 1), iota((8, LANES), 0)
    seg = seg_ref[...].astype(F32)
    wide = jnp.zeros((8, LANES), F32)
    for k in range(16):
        wide = jnp.where(lane8 // 8 == k, seg[:, k : k + 1], wide)
    own_lane = lane8 % 8 == sub8
    tile_row = jnp.sum(jnp.where(own_lane, wide, 0.0), axis=0, keepdims=True).astype(jnp.int32)
    owner_row = tile_row >> OWNER_SHIFT
    local_row = ((tile_row & ((1 << OWNER_SHIFT) - 1)) + 1).astype(F32)
    lane1 = iota((1, LANES), 1)
    start_row = (lane1 // 8) * LANES
    for d in range(DETS):
        start_row = jnp.where(lane1 % 8 == d, start_row - off_ref[d], start_row)
    start_row = start_row.astype(F32)
    det_row = (lane1 % 8).astype(F32)

    def spread_lanes(values):
        wide = jnp.zeros((values.shape[0], LANES), F32)
        lanes = iota(wide.shape, 1)
        for d in range(DETS):
            wide = jnp.where(lanes % 8 == d, values[:, d : d + 1], wide)
        return wide

    p_wide, r_wide = spread_lanes(p_ref[...]), spread_lanes(r_ref[...])
    vec_row = jnp.where(
        lane1 // 8 == META_P // 8,
        p_wide[0:1],
        jnp.where(
            lane1 // 8 == META_P // 8 + 1,
            p_wide[1:2],
            jnp.where(
                lane1 // 8 == META_R // 8, r_wide[0:1], jnp.where(lane1 // 8 == META_R // 8 + 1, r_wide[1:2], 0.0)
            ),
        ),
    )

    lane, sub = iota((RANKS, LANES), 1), iota((RANKS, LANES), 0)
    lane_f = lane.astype(F32)
    member = owner_row == sub
    first = jnp.min(jnp.where(member, lane_f, 512.0), axis=1, keepdims=True)
    last = jnp.max(jnp.where(member, lane_f, -1.0), axis=1, keepdims=True)
    pick0 = lane_f == first
    pick1 = (lane_f == last) & (last > first)
    hot0 = jnp.where(pick0, 1.0, 0.0).astype(BF16)
    hot1 = jnp.where(pick1, 1.0, 0.0).astype(BF16)
    cells = jnp.concatenate(
        [cell_ref[:, k * LANES : (k + 1) * LANES] for k in range(16)], axis=0
    ).astype(F32).astype(BF16)
    phases = jnp.concatenate([phase_ref[:, k * LANES : (k + 1) * LANES] for k in range(16)], axis=0)
    rows = dot(jnp.concatenate([hot0, hot1], axis=0), jnp.concatenate([cells, *split3(phases)], axis=1))
    phase_rows = rows[:, 128:256] + rows[:, 256:384] + rows[:, 384:512]
    meta = jnp.zeros((RANKS, LANES), F32) + vec_row
    column = 0
    for row in (local_row, start_row, det_row):
        for pick in (pick0, pick1):
            value = jnp.sum(jnp.where(pick, row, 0.0), axis=1, keepdims=True)
            meta = jnp.where(lane == column, value, meta)
            column += 1
    out_ref[pl.ds(0, RANKS, stride=PITCH), :] = rows[:RANKS, :128]
    out_ref[pl.ds(1, RANKS, stride=PITCH), :] = rows[RANKS:, :128]
    out_ref[pl.ds(2, RANKS, stride=PITCH), :] = phase_rows[:RANKS]
    out_ref[pl.ds(3, RANKS, stride=PITCH), :] = phase_rows[RANKS:]

    pl.semaphore_wait(barrier, RANKS)
    halos = []
    for side in range(2):
        dst = (me + 1) % RANKS if side == 0 else (me + RANKS - 1) % RANKS
        halos.append(
            pltpu.make_async_remote_copy(
                src_ref=p_ref,
                dst_ref=halo_ref.at[side],
                send_sem=halo_sem.at[side],
                recv_sem=halo_sem.at[2 + side],
                device_id={"tm": dst},
                device_id_type=MESH,
            )
        )
        halos[-1].start()
    for halo in halos:
        halo.wait()
    knots = spread_lanes(
        jnp.concatenate([halo_ref[0], p_ref[...], halo_ref[1], jnp.zeros((2, 8), F32)], axis=0)
    )
    parts = [part.astype(F32) for part in split3(knots)]
    table = jnp.concatenate(
        [
            jnp.concatenate(
                [jnp.zeros((META_E + 8 * s, LANES), F32), part, jnp.zeros((LANES - META_E - 8 * s - 8, LANES), F32)],
                axis=0,
            )
            for s in range(2)
            for part in parts
        ],
        axis=1,
    ).astype(BF16)
    out_ref[pl.ds(4, RANKS, stride=PITCH), :] = meta + dot_nt(jnp.concatenate([hot0, hot0, hot0, hot1, hot1, hot1], axis=1), table)

    def message(slot):
        return pl.ds(pl.multiple_of(slot * PITCH, PITCH), MSG)

    mine = pltpu.make_async_copy(out_ref.at[message(me)], own_ref.at[message(0)], in_sem.at[0])
    mine.start()

    def send(slot, dst, level):
        pltpu.make_async_remote_copy(
            src_ref=out_ref.at[message(dst)],
            dst_ref=own_ref.at[message(slot)],
            send_sem=send_sem,
            recv_sem=recv_sem.at[level],
            device_id={"tm": dst},
            device_id_type=MESH,
        ).start()

    def send_level(level, carry):
        each_target(send, level)(0)
        return carry

    each_target(send, 0)(1)
    lax.fori_loop(1, GROUPS, send_level, 0)
    mine.wait()

    def received(number, sem):
        return pltpu.make_async_remote_copy(
            src_ref=out_ref.at[pl.ds(0, number * MSG)],
            dst_ref=own_ref.at[pl.ds(0, number * MSG)],
            send_sem=send_sem,
            recv_sem=sem,
            device_id={"tm": me},
            device_id_type=MESH,
        )

    lane_b = iota((BLOCK, LANES), 1)
    lane_bf = lane_b.astype(F32)
    low_half = lane_b < 64
    pixel = (iota((64, LANES), 0) + 64 * core).astype(F32)

    def places(meta, s, lanes):
        u = meta[:, 2 + s : 3 + s] + lanes
        interval = jnp.floor(u * (1.0 / SPACING))
        fraction = (u - interval * SPACING) * (1.0 / SPACING)
        return interval, spline_weights(fraction)

    def process(ref, b, g):
        def field(k):
            return ref[pl.ds(g * BLOCK * PITCH + k, BLOCK, stride=PITCH), :]

        to = pl.ds(pl.multiple_of(b * RANKS + g * BLOCK, BLOCK), BLOCK)
        meta = field(4)
        for s in range(2):
            interval, weights = places(meta, s, lane_bf)
            early, late = interval < -0.5, interval > 0.5
            e = [meta[:, META_E + 8 * s + k : META_E + 8 * s + k + 1] for k in range(6)]
            stream = jnp.zeros((BLOCK, LANES), F32)
            for k in range(4):
                stream = stream + weights[k] * jnp.where(early, e[k], jnp.where(late, e[k + 2], e[k + 1]))
            c, sn = cos_sin(field(2 + s))
            stream_ref[s, to, :] = stream
            c_ref[s, to, :] = c
            s_ref[s, to, :] = sn
            channels = (stream, stream * c, stream * sn, jnp.ones_like(c), c, sn, c * c, c * sn, sn * sn)
            for ch, value in enumerate(channels):
                x_ref[s, pl.ds(ch, BLOCK, stride=16), :] = value
        cell0, cell1 = field(0), field(1)
        for j in range(BLOCK):
            hot = jnp.concatenate(
                [jnp.where(c[j : j + 1, :] == pixel, 1.0, 0.0) for c in (cell0, cell1)], axis=0
            ).astype(BF16)
            terms = jnp.concatenate(
                [part for s in range(2) for part in split2(x_ref[s, j * 16 : (j + 1) * 16, :])], axis=0
            )
            got = dot_nt(terms, hot)
            b_ref[j * 16 : (j + 1) * 16, :] = jnp.where(low_half, got[0:16] + got[16:32], got[32:48] + got[48:64])
        values = [b_ref[pl.ds(ch, BLOCK, stride=16), :] for ch in range(9)] + [jnp.zeros((BLOCK, LANES), F32)]
        turned = [pltpu.roll(value, 64, 1) for value in values]
        for pair in range(5):
            a, b2 = 2 * pair, 2 * pair + 1
            cols = slice(pair * 128, (pair + 1) * 128)
            both = (jnp.where(low_half, values[a], turned[b2]), jnp.where(low_half, turned[a], values[b2]))
            for s in range(2):
                for k, part in enumerate(split2(both[s])):
                    row = pl.multiple_of(k * 512 + s * 256 + b * RANKS + g * BLOCK, BLOCK)
                    bs_ref[pl.ds(row, BLOCK), cols] = part

    def pair_copy(g):
        at = pl.ds(pl.multiple_of(g * BLOCK * PITCH, BLOCK * PITCH), BLOCK * PITCH)
        return pltpu.make_async_remote_copy(
            src_ref=own_ref.at[at],
            dst_ref=par_ref.at[at],
            send_sem=pair_send.at[g],
            recv_sem=pair_recv.at[g],
            device_id={"det": 1 - core},
            device_id_type=MESH,
        )

    received(BLOCK - 1, recv_sem.at[0]).wait_recv()
    pair_copy(0).start()
    process(own_ref, 0, 0)

    def arrive(g, carry):
        received(BLOCK, recv_sem.at[g]).wait_recv()
        pair_copy(g).start()
        process(own_ref, 0, g)
        pair_copy(g - 1).wait_recv()
        process(par_ref, 1, g - 1)
        return carry

    lax.fori_loop(1, GROUPS, arrive, 0)
    pair_copy(GROUPS - 1).wait_recv()
    process(par_ref, 1, GROUPS - 1)

    metas = [ref[pl.ds(4, RANKS, stride=PITCH), :] for ref in (own_ref, par_ref)]
    turned = [value.T for value in metas]
    tile_rows = jnp.concatenate([turned[b][s : s + 1] for s in range(2) for b in range(2)], axis=1)

    for b in range(2):
        for s in range(2):
            same = jnp.where(metas[b][:, s : s + 1] == tile_rows, 1.0, 0.0).astype(BF16)
            t_ref[s, b * RANKS : (b + 1) * RANKS, :] = dot(jnp.concatenate([same, same], axis=1), bs_ref[...])

    ones = jnp.ones((2 * LANES, LANES), BF16)
    lane_s = iota((SUB, LANES), 1)
    lane_sf = lane_s.astype(F32)
    low_s = lane_s < 64

    def finish(ref, b, i):
        def field(k):
            return ref[pl.ds(i * SUB * PITCH + k, SUB, stride=PITCH), :]

        to = pl.ds(pl.multiple_of(b * RANKS + i * SUB, SUB), SUB)
        sums = []
        for pair in range(5):
            cols = slice(pair * 128, (pair + 1) * 128)
            t0, t1 = t_ref[0, to, cols], t_ref[1, to, cols]
            sums.append(jnp.where(low_s, t0, pltpu.roll(t1, 64, 1)))
            sums.append(jnp.where(low_s, pltpu.roll(t0, 64, 1), t1))
        maps = solve_pixels(tuple(sums[:9]))
        meta = field(4)
        out = jnp.zeros((SUB, LANES), F32)
        group = (core if b == 0 else 1 - core) * 8
        for s in range(2):
            cell = field(s).astype(jnp.int32)
            inside = (cell >> 6) == core
            index = (cell & 63) + 64 * s
            read = [jnp.take_along_axis(value, index, axis=1) for value in maps]
            cleaned = stream_ref[s, to, :] - (read[0] + c_ref[s, to, :] * read[1] + s_ref[s, to, :] * read[2])
            cleaned = jnp.where(inside, cleaned, 0.0)
            interval, weights = places(meta, s, lane_sf)
            terms = [weight * cleaned for weight in weights]
            detector = meta[:, 4 + s : 5 + s].astype(jnp.int32) + group
            values = []
            for col in range(6):
                value = jnp.zeros((SUB, LANES), F32)
                for k in range(4):
                    m = col - 1 - k
                    if -1 <= m <= 1:
                        value = value + jnp.where(interval == float(m), terms[k], 0.0)
                values.append(value)
            sums6 = dot(jnp.concatenate(split2(jnp.concatenate(values, axis=0)), axis=1), ones)
            for col in range(6):
                out = out + jnp.where(lane_s == detector + col * 16, sums6[col * SUB : (col + 1) * SUB], 0.0)
        return out

    def finish_rows(i, carry):
        total = finish(own_ref, 0, i) + finish(par_ref, 1, i)
        for k, part in enumerate(split3(total)):
            v_ref[pl.ds(pl.multiple_of(k * RANKS + i * SUB, SUB), SUB), :] = part
        return carry

    lax.fori_loop(0, RANKS // SUB, finish_rows, 0)

    dy, dx, dz = steps(lane)
    sender = (((y - dy + NY) % NY) * NX + (x - dx + NX) % NX) * NZ + (z - dz + NZ) % NZ
    order = jnp.where(sender == sub, 1.0, 0.0).astype(BF16)
    order3 = jnp.concatenate([order] * 3, axis=1)
    image = dot(order3, v_ref[...]).T
    for g in range(2):
        for n in range(2):
            def image_rows(c):
                return image[c * 16 + g * 8 : c * 16 + g * 8 + 8]
            value = (
                image_rows(2 + n) + pltpu.roll(image_rows(n), RANKS - 1, 1) + pltpu.roll(image_rows(4 + n), 1, 1)
            )
            part_ref[g * 16 + n * 8 : g * 16 + n * 8 + 8, :] = value

    here = pl.ds(pl.multiple_of(core * 16, 16), 16)
    there = pl.ds(pl.multiple_of((1 - core) * 16, 16), 16)

    def swap(src, dst, k):
        return pltpu.make_async_remote_copy(
            src_ref=src,
            dst_ref=dst,
            send_sem=red_send.at[k],
            recv_sem=red_recv.at[k],
            device_id={"det": 1 - core},
            device_id_type=MESH,
        )

    swapped = swap(part_ref.at[there], first_ref, 0)
    swapped.start()
    both = []
    for b in range(2):
        sorted_meta = dot(order3, jnp.concatenate(split3(metas[b]), axis=0)).T
        both.append(sorted_meta[META_P : META_P + 32])
    p_full = jnp.where(
        core == 0,
        jnp.concatenate([both[0][0:16], both[1][0:16]], axis=0),
        jnp.concatenate([both[1][0:16], both[0][0:16]], axis=0),
    )
    r_full = jnp.where(
        core == 0,
        jnp.concatenate([both[0][16:32], both[1][16:32]], axis=0),
        jnp.concatenate([both[1][16:32], both[0][16:32]], axis=0),
    )

    def total_of(value):
        return jnp.sum(jnp.sum(value, axis=1, keepdims=True), axis=0, keepdims=True)

    norm_old = total_of(r_full * r_full)
    swapped.wait()
    total = part_ref[here, :] + first_ref[...]
    for stage, ((size, stride), buf) in enumerate(zip(LEVELS, (lz_ref, ly_ref, lx_ref))):
        at = (me // stride) % size
        hold_ref[stage] = total
        buf[at] = total
        for step in range(1, size):
            pltpu.make_async_remote_copy(
                src_ref=hold_ref.at[stage],
                dst_ref=buf.at[at],
                send_sem=red_send.at[1 + stage],
                recv_sem=red_recv.at[1 + stage],
                device_id={"tm": me + ((at + step) % size - at) * stride},
                device_id_type=MESH,
            ).start()
        rest = pltpu.make_async_remote_copy(
            src_ref=buf.at[pl.ds(0, size - 1)],
            dst_ref=buf.at[pl.ds(0, size - 1)],
            send_sem=red_send.at[1 + stage],
            recv_sem=red_recv.at[1 + stage],
            device_id={"tm": me},
            device_id_type=MESH,
        )
        rest.wait_recv()
        rest.wait_send()
        total = buf[0]
        for k in range(1, size):
            total = total + buf[k]
    hold_ref[3] = total
    full_ref[here, :] = total
    swapped = swap(hold_ref.at[3], full_ref.at[here], 4)
    swapped.start()
    swapped.wait()
    received(RANKS - 1, recv_sem.at[0]).wait_send()

    def sent(g, carry):
        pair_copy(g).wait_send()
        return carry

    lax.fori_loop(0, GROUPS, sent, 0)

    image = full_ref[...] * (1.0 / SPACING) + BASE_PRIOR * p_full
    alpha = norm_old / total_of(p_full * image)
    fresh = r_full - alpha * image
    beta = total_of(fresh * fresh) / norm_old
    column = jnp.sum(jnp.where(iota((32, LANES), 1) == me, image, 0.0), axis=1, keepdims=True)
    column = jnp.where(core == 0, column[0:16], column[16:32])
    local = jnp.concatenate(
        [
            jnp.sum(jnp.where(lane8 == sub8, column[n * 8 : n * 8 + 8], 0.0), axis=0, keepdims=True)
            for n in range(2)
        ],
        axis=0,
    )[:, 0:DETS]
    search = p_ref[...]
    fresh_own = r_ref[...] - alpha * local
    x_out[...] = off_in_ref[...] + alpha * search
    r_out[...] = fresh_own
    p_out[...] = fresh_own + beta * search


def body(offsets, residual, search, lattice, cells, phases, tiles):
    anywhere = pl.BlockSpec(memory_space=pl.ANY)
    message = (RANKS * PITCH, LANES)
    small = jax.ShapeDtypeStruct((2, DETS), F32)
    outs = pl.pallas_call(
        destripe_kernel,
        out_shape=(small,) * 3,
        in_specs=[pl.BlockSpec(memory_space=pltpu.SMEM)] + [anywhere] * 6,
        out_specs=(pl.BlockSpec(memory_space=pltpu.VMEM),) * 3,
        scratch_shapes=[
            pltpu.VMEM((8, 16), jnp.int32),
            pltpu.VMEM((8, 2048), jnp.int32),
            pltpu.VMEM((8, 2048), F32),
            pltpu.VMEM((2, 8), F32),
            pltpu.VMEM((2, 8), F32),
            pltpu.VMEM((2, 8), F32),
            pltpu.VMEM((2, 2, 8), F32),
            pltpu.VMEM(message, F32),
            pltpu.VMEM(message, F32),
            pltpu.VMEM(message, F32),
            pltpu.VMEM((2, BLOCK * 16, LANES), F32),
            pltpu.VMEM((BLOCK * 16, LANES), F32),
            pltpu.VMEM((1024, 640), BF16),
            pltpu.VMEM((2, COUNT, 640), F32),
            pltpu.VMEM((2, COUNT, LANES), F32),
            pltpu.VMEM((2, COUNT, LANES), F32),
            pltpu.VMEM((2, COUNT, LANES), F32),
            pltpu.VMEM((3 * RANKS, LANES), BF16),
            pltpu.VMEM((32, LANES), F32),
            pltpu.VMEM((16, LANES), F32),
            pltpu.VMEM((4, 16, LANES), F32),
            pltpu.VMEM((NZ, 16, LANES), F32),
            pltpu.VMEM((NY, 16, LANES), F32),
            pltpu.VMEM((NX, 16, LANES), F32),
            pltpu.VMEM((32, LANES), F32),
            pltpu.SemaphoreType.DMA((6,)),
            pltpu.SemaphoreType.DMA((4,)),
            pltpu.SemaphoreType.DMA,
            pltpu.SemaphoreType.DMA((GROUPS,)),
            pltpu.SemaphoreType.DMA((GROUPS,)),
            pltpu.SemaphoreType.DMA((GROUPS,)),
            pltpu.SemaphoreType.DMA((5,)),
            pltpu.SemaphoreType.DMA((5,)),
        ],
        compiler_params=pltpu.CompilerParams(collective_id=0, has_side_effects=True),
        name="destripe",
    )(lattice, tiles, cells, phases, search.T, residual.T, offsets.T)
    return tuple(out.T for out in outs)


def solution(mesh):
    return jax.shard_map(
        body,
        mesh=mesh,
        in_specs=(
            P("det", "tm"),
            P("det", "tm"),
            P("det", "tm"),
            P("det"),
            P("det", "tm"),
            P("det", "tm"),
            P("det", "tm"),
        ),
        out_specs=(P("det", "tm"), P("det", "tm"), P("det", "tm")),
        check_vma=False,
    )
```

time: 399 us -> 55.8 us (0.14)
  blocking collectives: 151 us -> 0 us
  waiting for transfers between devices: 85 us -> 0 us
  starting transfers between devices: 53.3 us -> 0 us
  Pallas kernels: 0 us -> 52.5 us
  other arithmetic: 41.5 us -> 0 us
  local copies, waits for them, and re-layouts: 33 us -> 2.49 us
  between operations: 17.1 us -> 0.65 us
  matrix products: 15.4 us -> 0 us
    psum x2 -> x0, blocking collectives: 151 us -> none  [the longest x1 77.8 us: body(): norm_old = lax.psum(jnp.sum(leftover_error * leftover_error), ('tm', 'det'))]
    pallas_call x0 -> x1, Pallas kernels: none -> 52.5 us  [body(): pl.pallas_call(destripe_kernel, out_shape=(small,) * 3, in_specs=[pl.Bloc...]
    all_to_all x3 -> x0, waiting for transfers between devices: 47.3 us -> none  [the longest x1 31.4 us: body(): lax.all_to_all(outgoing.reshape(ranks, capacity, 9, LANES), 'tm', split_a...]
    psum x1 -> x0, waiting for transfers between devices: 36.8 us -> none  [combine_maps(): totals = lax.psum(partial_value, 'det')]
    all_to_all x3 -> x0, starting transfers between devices: 34.9 us -> none  [the longest x1 13.8 us: body(): lax.all_to_all(returned, 'tm', split_axis=0, concat_axis=0, tiled=True)]
    scatter-add x1 -> x0, other arithmetic: 30.1 us -> none  [place_rows(): jnp.zeros((owner_tiles + 1, 9, LANES), jnp.float32).at[targets].add(rows)]
    ppermute x4 -> x0, starting transfers between devices: 18.2 us -> none  [the longest x2 14.8 us: padded_2(): lax.ppermute(head, axis, [((i + 1) % count, i) for i in range(count)])]
    dot_general x4 -> x0, matrix products: 15.4 us -> none  [the longest x2 8.09 us: read_one_group(): jnp.einsum('rhe,roe->rho', input_arrays[0], indicator_matrix, precision=l...]
  transfers between devices with their start and end apart: 8 -> 0, of which waited for: 4 -> 0; matrix products, arithmetic and copies ran while one was open for 7% -> 0% of each run, Pallas kernels for 0% -> 0%
where the time goes in v2:
time: 55.8 us; the launch traced here: 55.7 us
  Pallas kernels  52.5 us (94%)
  local copies, waits for them, and re-layouts  2.49 us (4%)
  between operations  0.65 us (1%)
    pallas_call x1, Pallas kernels, body(): pl.pallas_call(destripe_kernel, out_shape=(small,) * 3, in_specs=[pl.Bloc...  52.5 us
    unnamed x9, local copies, waits for them, and re-layouts  2.49 us

profile of v2, /device:TPU:1, one launch (start us, length us, event | category | flops | bytes accessed | tf_op | source)
XLA Modules:
  0.0 55.7 jit_solution(6554315793903026774)
XLA Ops:
  0.6 52.5 %destripe.1 = (f32[2,8]{1,0:T(2,128)}, f32[2,8]{1,0:T(2,128)}, f32[2,8]{1,0:T(2,128)}) custom-call(s32[8]{0:T(128)} %off_ref.1, s32[8,16]{1,0:T(8,128)} %seg_hbm.1, s32[8,2048]{1,0:T(8,128)} %cell_hbm.1, f32[8,2048]{1,0:T(8,128)} %phase_hbm.1, f32[2,8]{1,0:T(2,128)} %bitcast.6, f32[2,8]{1,0:T(2,128)} %bitcast.7, f32[2,8]{1,0:T(2,128)} %bitcast.8), custom_call_target="tpu_custom_call" | custom-call | tf_op jit(solution)/shard_map/destripe/pallas_call | solution.py:546
  53.2 0.0 copy-start.2
  53.2 0.6 %copy-done.2 = f32[2,8]{1,0:T(2,128)S(1)} copy-done((f32[2,8]{1,0:T(2,128)S(1)}, f32[2,8]{1,0:T(2,128)}, u32[]{:S(2)}) %copy-start.2) | copy-done | bytes 88
  53.8 0.0 copy-start.1
  53.8 0.6 %copy.13 = f32[8,2]{0,1:T(2,128)} copy(f32[8,2]{0,1:T(2,128)S(1)} %bitcast.11) | data formatting | bytes 128
  54.4 0.1 copy-done.1
  54.4 0.0 copy-start
  54.4 0.6 %copy.14 = f32[8,2]{0,1:T(2,128)} copy(f32[8,2]{0,1:T(2,128)S(1)} %bitcast.10) | data formatting | bytes 128
  55.0 0.1 copy-done
  55.1 0.6 %copy.15 = f32[8,2]{0,1:T(2,128)} copy(f32[8,2]{0,1:T(2,128)S(1)} %bitcast.9) | data formatting | bytes 128
Async XLA Ops:
  53.2 0.6 %copy-start.2 = (f32[2,8]{1,0:T(2,128)S(1)}, f32[2,8]{1,0:T(2,128)}, u32[]{:S(2)}) copy-start(f32[2,8]{1,0:T(2,128)} %get-tuple-element.6) | copy-start | bytes 196
  53.8 0.6 %copy-start.1 = (f32[2,8]{1,0:T(2,128)S(1)}, f32[2,8]{1,0:T(2,128)}, u32[]{:S(2)}) copy-start(f32[2,8]{1,0:T(2,128)} %get-tuple-element.7) | copy-start | bytes 196
  54.4 0.7 %copy-start = (f32[2,8]{1,0:T(2,128)S(1)}, f32[2,8]{1,0:T(2,128)}, u32[]{:S(2)}) copy-start(f32[2,8]{1,0:T(2,128)} %get-tuple-element.8) | copy-start | bytes 196

commit v3 on v2

--- a/solution.py
+++ b/solution.py
@@ -114,7 +114,7 @@
 
 
 def destripe_kernel(
-    off_ref, seg_hbm, cell_hbm, phase_hbm, p_hbm, r_hbm, o_hbm, x_out, r_out, p_out, seg_ref, cell_ref, phase_ref, p_ref, r_ref, off_in_ref, halo_ref, out_ref, own_ref, par_ref, x_ref, b_ref, bs_ref, t_ref, stream_ref, c_ref, s_ref, v_ref, part_ref, first_ref, hold_ref, lz_ref, ly_ref, lx_ref, full_ref, in_sem, halo_sem, send_sem, recv_sem, pair_send, pair_recv, red_send, red_recv
+    off_ref, seg_hbm, cell_hbm, phase_hbm, p_hbm, r_hbm, o_hbm, x_out, r_out, p_out, seg_ref, cell_ref, phase_ref, p_ref, r_ref, off_in_ref, halo_ref, out_ref, own_ref, par_ref, x_ref, b_ref, bs_ref, t_ref, stream_ref, c_ref, s_ref, v_ref, part_ref, first_ref, hold_ref, lz_ref, ly_ref, lx_ref, in_sem, halo_sem, send_sem, recv_sem, pair_send, pair_recv, red_send, red_recv
 ):
     me = lax.axis_index("tm")
     core = lax.axis_index("det")
@@ -148,6 +148,9 @@
     lax.fori_loop(1, GROUPS, greet_level, 0)
     each_target(greet, 0)(1)
     pl.semaphore_signal(barrier, inc=1, device_id={"det": 1 - core}, device_id_type=MESH)
+    across = [me + ((x + step) % NX - x) * NZ for step in range(1, NX)]
+    for dst in across:
+        pl.semaphore_signal(barrier, inc=1, device_id={"tm": dst, "det": 1 - core}, device_id_type=MESH)
 
     loads = [
         pltpu.make_async_copy(a, b, in_sem.at[k])
@@ -223,7 +226,7 @@
     out_ref[pl.ds(2, RANKS, stride=PITCH), :] = phase_rows[:RANKS]
     out_ref[pl.ds(3, RANKS, stride=PITCH), :] = phase_rows[RANKS:]
 
-    pl.semaphore_wait(barrier, RANKS)
+    pl.semaphore_wait(barrier, RANKS + NX - 1)
     halos = []
     for side in range(2):
         dst = (me + 1) % RANKS if side == 0 else (me + RANKS - 1) % RANKS
@@ -294,7 +297,9 @@
     lane_b = iota((BLOCK, LANES), 1)
     lane_bf = lane_b.astype(F32)
     low_half = lane_b < 64
-    pixel = (iota((64, LANES), 0) + 64 * core).astype(F32)
+    pixel = (iota((64, LANES), 0) + 64 * core).astype(F32).astype(BF16)
+
+    one, zero = jnp.ones((), BF16), jnp.zeros((), BF16)
 
     def places(meta, s, lanes):
         u = meta[:, 2 + s : 3 + s] + lanes
@@ -321,18 +326,22 @@
             s_ref[s, to, :] = sn
             channels = (stream, stream * c, stream * sn, jnp.ones_like(c), c, sn, c * c, c * sn, sn * sn)
             for ch, value in enumerate(channels):
-                x_ref[s, pl.ds(ch, BLOCK, stride=16), :] = value
+                x_ref[2 * b + s, pl.ds(ch, BLOCK, stride=16), :] = value
         cell0, cell1 = field(0), field(1)
         for j in range(BLOCK):
             hot = jnp.concatenate(
-                [jnp.where(c[j : j + 1, :] == pixel, 1.0, 0.0) for c in (cell0, cell1)], axis=0
-            ).astype(BF16)
+                [
+                    jnp.where(jnp.broadcast_to(c[j : j + 1, :].astype(BF16), (64, LANES)) == pixel, one, zero)
+                    for c in (cell0, cell1)
+                ],
+                axis=0,
+            )
             terms = jnp.concatenate(
-                [part for s in range(2) for part in split2(x_ref[s, j * 16 : (j + 1) * 16, :])], axis=0
+                [part for s in range(2) for part in split2(x_ref[2 * b + s, j * 16 : (j + 1) * 16, :])], axis=0
             )
             got = dot_nt(terms, hot)
-            b_ref[j * 16 : (j + 1) * 16, :] = jnp.where(low_half, got[0:16] + got[16:32], got[32:48] + got[48:64])
-        values = [b_ref[pl.ds(ch, BLOCK, stride=16), :] for ch in range(9)] + [jnp.zeros((BLOCK, LANES), F32)]
+            b_ref[b, j * 16 : (j + 1) * 16, :] = jnp.where(low_half, got[0:16] + got[16:32], got[32:48] + got[48:64])
+        values = [b_ref[b, pl.ds(ch, BLOCK, stride=16), :] for ch in range(9)] + [jnp.zeros((BLOCK, LANES), F32)]
         turned = [pltpu.roll(value, 64, 1) for value in values]
         for pair in range(5):
             a, b2 = 2 * pair, 2 * pair + 1
@@ -361,8 +370,8 @@
     def arrive(g, carry):
         received(BLOCK, recv_sem.at[g]).wait_recv()
         pair_copy(g).start()
+        pair_copy(g - 1).wait_recv()
         process(own_ref, 0, g)
-        pair_copy(g - 1).wait_recv()
         process(par_ref, 1, g - 1)
         return carry
 
@@ -408,18 +417,15 @@
             cleaned = jnp.where(inside, cleaned, 0.0)
             interval, weights = places(meta, s, lane_sf)
             terms = [weight * cleaned for weight in weights]
-            detector = meta[:, 4 + s : 5 + s].astype(jnp.int32) + group
-            values = []
-            for col in range(6):
-                value = jnp.zeros((SUB, LANES), F32)
-                for k in range(4):
-                    m = col - 1 - k
-                    if -1 <= m <= 1:
-                        value = value + jnp.where(interval == float(m), terms[k], 0.0)
-                values.append(value)
-            sums6 = dot(jnp.concatenate(split2(jnp.concatenate(values, axis=0)), axis=1), ones)
-            for col in range(6):
-                out = out + jnp.where(lane_s == detector + col * 16, sums6[col * SUB : (col + 1) * SUB], 0.0)
+            early = jnp.floor(meta[:, 2 + s : 3 + s] * (1.0 / SPACING))
+            head = interval == early
+            values = [jnp.where(head, terms[0], 0.0)]
+            values += [jnp.where(head, terms[k], terms[k - 1]) for k in range(1, 4)]
+            values.append(jnp.where(head, 0.0, terms[3]))
+            spot = (meta[:, 4 + s : 5 + s] + (early + 1.0) * 16.0).astype(jnp.int32) + group
+            sums5 = dot(jnp.concatenate(split2(jnp.concatenate(values, axis=0)), axis=1), ones)
+            for k in range(5):
+                out = out + jnp.where(lane_s - 16 * k == spot, sums5[k * SUB : (k + 1) * SUB], 0.0)
         return out
 
     def finish_rows(i, carry):
@@ -480,7 +486,7 @@
     norm_old = total_of(r_full * r_full)
     swapped.wait()
     total = part_ref[here, :] + first_ref[...]
-    for stage, ((size, stride), buf) in enumerate(zip(LEVELS, (lz_ref, ly_ref, lx_ref))):
+    for stage, ((size, stride), buf) in enumerate(zip(LEVELS, (lz_ref, ly_ref))):
         at = (me // stride) % size
         hold_ref[stage] = total
         buf[at] = total
@@ -502,15 +508,39 @@
             device_id_type=MESH,
         )
         rest.wait_recv()
-        rest.wait_send()
         total = buf[0]
         for k in range(1, size):
             total = total + buf[k]
-    hold_ref[3] = total
-    full_ref[here, :] = total
-    swapped = swap(hold_ref.at[3], full_ref.at[here], 4)
+        rest.wait_send()
+    hold_ref[2] = total
+    lx_ref[x, here, :] = total
+    for dst in across:
+        for det in (core, 1 - core):
+            pltpu.make_async_remote_copy(
+                src_ref=hold_ref.at[2],
+                dst_ref=lx_ref.at[x, here],
+                send_sem=red_send.at[3],
+                recv_sem=red_recv.at[3],
+                device_id={"tm": dst, "det": det},
+                device_id_type=MESH,
+            ).start()
+    swapped = swap(hold_ref.at[2], lx_ref.at[x, here], 4)
     swapped.start()
-    swapped.wait()
+    rest = pltpu.make_async_remote_copy(
+        src_ref=lx_ref.at[pl.ds(0, NX - 1)],
+        dst_ref=lx_ref.at[pl.ds(0, NX - 1)],
+        send_sem=red_send.at[3],
+        recv_sem=red_recv.at[3],
+        device_id={"tm": me},
+        device_id_type=MESH,
+    )
+    rest.wait_recv()
+    swapped.wait_recv()
+    total = lx_ref[0]
+    for k in range(1, NX):
+        total = total + lx_ref[k]
+    rest.wait_send()
+    swapped.wait_send()
     received(RANKS - 1, recv_sem.at[0]).wait_send()
 
     def sent(g, carry):
@@ -519,7 +549,7 @@
 
     lax.fori_loop(0, GROUPS, sent, 0)
 
-    image = full_ref[...] * (1.0 / SPACING) + BASE_PRIOR * p_full
+    image = total * (1.0 / SPACING) + BASE_PRIOR * p_full
     alpha = norm_old / total_of(p_full * image)
     fresh = r_full - alpha * image
     beta = total_of(fresh * fresh) / norm_old
@@ -542,10 +572,9 @@
 def body(offsets, residual, search, lattice, cells, phases, tiles):
     anywhere = pl.BlockSpec(memory_space=pl.ANY)
     message = (RANKS * PITCH, LANES)
-    small = jax.ShapeDtypeStruct((2, DETS), F32)
     outs = pl.pallas_call(
         destripe_kernel,
-        out_shape=(small,) * 3,
+        out_shape=(pltpu.VMEM((2, DETS), F32),) * 3,
         in_specs=[pl.BlockSpec(memory_space=pltpu.SMEM)] + [anywhere] * 6,
         out_specs=(pl.BlockSpec(memory_space=pltpu.VMEM),) * 3,
         scratch_shapes=[
@@ -559,8 +588,8 @@
             pltpu.VMEM(message, F32),
             pltpu.VMEM(message, F32),
             pltpu.VMEM(message, F32),
+            pltpu.VMEM((4, BLOCK * 16, LANES), F32),
             pltpu.VMEM((2, BLOCK * 16, LANES), F32),
-            pltpu.VMEM((BLOCK * 16, LANES), F32),
             pltpu.VMEM((1024, 640), BF16),
             pltpu.VMEM((2, COUNT, 640), F32),
             pltpu.VMEM((2, COUNT, LANES), F32),
@@ -572,8 +601,7 @@
             pltpu.VMEM((4, 16, LANES), F32),
             pltpu.VMEM((NZ, 16, LANES), F32),
             pltpu.VMEM((NY, 16, LANES), F32),
-            pltpu.VMEM((NX, 16, LANES), F32),
-            pltpu.VMEM((32, LANES), F32),
+            pltpu.VMEM((NX, 32, LANES), F32),
             pltpu.SemaphoreType.DMA((6,)),
             pltpu.SemaphoreType.DMA((4,)),
             pltpu.SemaphoreType.DMA,

time: 55.8 us -> 51.6 us (0.925)
  Pallas kernels: 52.5 us -> 49.1 us
  local copies, waits for them, and re-layouts: 2.49 us -> 1.69 us
    pallas_call x1, Pallas kernels: 52.5 us -> 49.1 us  [body(): pl.pallas_call(destripe_kernel, out_shape=(pltpu.VMEM((2, DETS), F32),) *...]
    unnamed x9 -> x3, local copies, waits for them, and re-layouts: 2.49 us -> 1.69 us
where the time goes in v3:
time: 51.6 us; the launch traced here: 51.5 us
  Pallas kernels  49.1 us (95%)
  local copies, waits for them, and re-layouts  1.69 us (3%)
  between operations  0.64 us (1%)
    pallas_call x1, Pallas kernels, body(): pl.pallas_call(destripe_kernel, out_shape=(pltpu.VMEM((2, DETS), F32),) *...  49.1 us
    unnamed x3, local copies, waits for them, and re-layouts  1.69 us

profile of v3, /device:TPU:1, one launch (start us, length us, event | category | flops | bytes accessed | tf_op | source)
XLA Modules:
  0.0 51.5 jit_solution(17666470707545449133)
XLA Ops:
  0.6 49.1 %destripe.1 = (f32[2,8]{1,0:T(2,128)S(1)}, f32[2,8]{1,0:T(2,128)S(1)}, f32[2,8]{1,0:T(2,128)S(1)}) custom-call(s32[8]{0:T(128)} %off_ref.1, s32[8,16]{1,0:T(8,128)} %seg_hbm.1, s32[8,2048]{1,0:T(8,128)} %cell_hbm.1, f32[8,2048]{1,0:T(8,128)} %phase_hbm.1, f32[2,8]{1,0:T(2,128)} %bitcast.9, f32[2,8]{1,0:T(2,128)} %bitcast.10, f32[2,8]{1,0:T(2,128)} %bitcast.11), custom_call_target="tpu_custom_call" | custom-call | tf_op jit(solution)/shard_map/destripe/pallas_call | solution.py:575
  49.8 0.6 %copy.13 = f32[8,2]{0,1:T(2,128)} copy(f32[8,2]{0,1:T(2,128)S(1)} %bitcast.8) | data formatting | bytes 128
  50.3 0.6 %copy.14 = f32[8,2]{0,1:T(2,128)} copy(f32[8,2]{0,1:T(2,128)S(1)} %bitcast.7) | data formatting | bytes 128
  50.9 0.6 %copy.15 = f32[8,2]{0,1:T(2,128)} copy(f32[8,2]{0,1:T(2,128)S(1)} %bitcast.6) | data formatting | bytes 128

commit v4 on v3

--- a/solution.py
+++ b/solution.py
@@ -100,7 +100,7 @@
 COUNT = 2 * RANKS
 BLOCK = 16
 GROUPS = RANKS // BLOCK
-SUB = 64
+SUB = 128
 META_E, META_P, META_R = 16, 32, 48
 LEVELS = ((NZ, 1), (NY, NX * NZ), (NX, NZ))
 

time: 51.6 us -> 50.4 us (0.977)
  Pallas kernels: 49.1 us -> 48 us
    pallas_call x1, Pallas kernels: 49.1 us -> 48 us  [body(): pl.pallas_call(destripe_kernel, out_shape=(pltpu.VMEM((2, DETS), F32),) *...]
where the time goes in v4:
time: 50.4 us; the launch traced here: 50.3 us
  Pallas kernels  48 us (95%)
  local copies, waits for them, and re-layouts  1.69 us (3%)
  between operations  0.64 us (1%)
    pallas_call x1, Pallas kernels, body(): pl.pallas_call(destripe_kernel, out_shape=(pltpu.VMEM((2, DETS), F32),) *...  48 us
    unnamed x3, local copies, waits for them, and re-layouts  1.69 us

profile of v4, /device:TPU:1, one launch (start us, length us, event | category | flops | bytes accessed | tf_op | source)
XLA Modules:
  0.0 50.3 jit_solution(4899598650382519464)
XLA Ops:
  0.6 48.0 %destripe.1 = (f32[2,8]{1,0:T(2,128)S(1)}, f32[2,8]{1,0:T(2,128)S(1)}, f32[2,8]{1,0:T(2,128)S(1)}) custom-call(s32[8]{0:T(128)} %off_ref.1, s32[8,16]{1,0:T(8,128)} %seg_hbm.1, s32[8,2048]{1,0:T(8,128)} %cell_hbm.1, f32[8,2048]{1,0:T(8,128)} %phase_hbm.1, f32[2,8]{1,0:T(2,128)} %bitcast.9, f32[2,8]{1,0:T(2,128)} %bitcast.10, f32[2,8]{1,0:T(2,128)} %bitcast.11), custom_call_target="tpu_custom_call" | custom-call | tf_op jit(solution)/shard_map/destripe/pallas_call | solution.py:575
  48.6 0.6 %copy.13 = f32[8,2]{0,1:T(2,128)} copy(f32[8,2]{0,1:T(2,128)S(1)} %bitcast.8) | data formatting | bytes 128
  49.2 0.6 %copy.14 = f32[8,2]{0,1:T(2,128)} copy(f32[8,2]{0,1:T(2,128)S(1)} %bitcast.7) | data formatting | bytes 128
  49.7 0.6 %copy.15 = f32[8,2]{0,1:T(2,128)} copy(f32[8,2]{0,1:T(2,128)S(1)} %bitcast.6) | data formatting | bytes 128

commit v5 on v4

--- a/solution.py
+++ b/solution.py
@@ -571,7 +571,7 @@
 
 def body(offsets, residual, search, lattice, cells, phases, tiles):
     anywhere = pl.BlockSpec(memory_space=pl.ANY)
-    message = (RANKS * PITCH, LANES)
+    message = (RANKS * PITCH + PITCH, LANES)
     outs = pl.pallas_call(
         destripe_kernel,
         out_shape=(pltpu.VMEM((2, DETS), F32),) * 3,
@@ -588,8 +588,8 @@
             pltpu.VMEM(message, F32),
             pltpu.VMEM(message, F32),
             pltpu.VMEM(message, F32),
-            pltpu.VMEM((4, BLOCK * 16, LANES), F32),
-            pltpu.VMEM((2, BLOCK * 16, LANES), F32),
+            pltpu.VMEM((4, BLOCK * 16 + 16, LANES), F32),
+            pltpu.VMEM((2, BLOCK * 16 + 16, LANES), F32),
             pltpu.VMEM((1024, 640), BF16),
             pltpu.VMEM((2, COUNT, 640), F32),
             pltpu.VMEM((2, COUNT, LANES), F32),

time: 50.4 us -> 50.4 us (level)
  no operation moved by 1% of the time
where the time goes in v5:
time: 50.4 us; the launch traced here: 50.3 us
  Pallas kernels  48 us (95%)
  local copies, waits for them, and re-layouts  1.69 us (3%)
  between operations  0.64 us (1%)
    pallas_call x1, Pallas kernels, body(): pl.pallas_call(destripe_kernel, out_shape=(pltpu.VMEM((2, DETS), F32),) *...  48 us
    unnamed x3, local copies, waits for them, and re-layouts  1.69 us

profile of v5, /device:TPU:1, one launch (start us, length us, event | category | flops | bytes accessed | tf_op | source)
XLA Modules:
  0.0 50.3 jit_solution(16368125687157390534)
XLA Ops:
  0.6 48.0 %destripe.1 = (f32[2,8]{1,0:T(2,128)S(1)}, f32[2,8]{1,0:T(2,128)S(1)}, f32[2,8]{1,0:T(2,128)S(1)}) custom-call(s32[8]{0:T(128)} %off_ref.1, s32[8,16]{1,0:T(8,128)} %seg_hbm.1, s32[8,2048]{1,0:T(8,128)} %cell_hbm.1, f32[8,2048]{1,0:T(8,128)} %phase_hbm.1, f32[2,8]{1,0:T(2,128)} %bitcast.9, f32[2,8]{1,0:T(2,128)} %bitcast.10, f32[2,8]{1,0:T(2,128)} %bitcast.11), custom_call_target="tpu_custom_call" | custom-call | tf_op jit(solution)/shard_map/destripe/pallas_call | solution.py:575
  48.6 0.6 %copy.13 = f32[8,2]{0,1:T(2,128)} copy(f32[8,2]{0,1:T(2,128)S(1)} %bitcast.8) | data formatting | bytes 128
  49.2 0.6 %copy.14 = f32[8,2]{0,1:T(2,128)} copy(f32[8,2]{0,1:T(2,128)S(1)} %bitcast.7) | data formatting | bytes 128
  49.7 0.6 %copy.15 = f32[8,2]{0,1:T(2,128)} copy(f32[8,2]{0,1:T(2,128)S(1)} %bitcast.6) | data formatting | bytes 128
